TPU v7x, 32 devices: a whole 2x2x4 slice. The times are simulated.
32 devices in a mesh: xi: 8 (over z, core), eta: 4 (over y, x).
Axes of the slice: x: 2, y: 2, z: 4, core: 2. Of those that a mesh axis runs over, the one named last changes fastest.
Arguments:
- mantle_disp: float32 [3, 36, 2160], P(None, 'eta', 'xi'), may hold values from -6 to 6
- mantle_vel: float32 [3, 36, 2160], P(None, 'eta', 'xi'), may hold values from -6 to 6
- mantle_acc: float32 [3, 36, 2160], P(None, 'eta', 'xi'), may hold values from -12 to 12
- mantle_metric: float32 [3, 36, 2160], P(None, 'eta', 'xi'), may hold values from 0.7 to 1.4
- mantle_moduli: float32 [2, 36, 2160], P(None, 'eta', 'xi'), may hold values from 0.02 to 0.2
- mantle_rho: float32 [36, 2160], P('eta', 'xi'), may hold values from 0.5 to 2
- core_pot: float32 [36, 2160], P('eta', 'xi'), may hold values from -6 to 6
- core_rate: float32 [36, 2160], P('eta', 'xi'), may hold values from -6 to 6
- core_accel: float32 [36, 2160], P('eta', 'xi'), may hold values from -12 to 12
- core_metric: float32 [3, 36, 2160], P(None, 'eta', 'xi'), may hold values from 0.7 to 1.4
- core_kappa: float32 [36, 2160], P('eta', 'xi'), may hold values from 0.02 to 0.2
- core_rho: float32 [36, 2160], P('eta', 'xi'), may hold values from 0.5 to 2
- inner_disp: float32 [3, 36, 1200], P(None, 'eta', 'xi'), may hold values from -6 to 6
- inner_vel: float32 [3, 36, 1200], P(None, 'eta', 'xi'), may hold values from -6 to 6
- inner_acc: float32 [3, 36, 1200], P(None, 'eta', 'xi'), may hold values from -12 to 12
- inner_metric: float32 [3, 36, 1200], P(None, 'eta', 'xi'), may hold values from 0.7 to 1.4
- inner_moduli: float32 [2, 36, 1200], P(None, 'eta', 'xi'), may hold values from 0.02 to 0.2
- inner_rho: float32 [36, 1200], P('eta', 'xi'), may hold values from 0.5 to 2
Outputs:
- mantle_disp_new: float32 [3, 36, 2160], P(None, 'eta', 'xi')
- mantle_vel_new: float32 [3, 36, 2160], P(None, 'eta', 'xi')
- mantle_acc_new: float32 [3, 36, 2160], P(None, 'eta', 'xi')
- core_pot_new: float32 [36, 2160], P('eta', 'xi')
- core_rate_new: float32 [36, 2160], P('eta', 'xi')
- core_accel_new: float32 [36, 2160], P('eta', 'xi')
- inner_disp_new: float32 [3, 36, 1200], P(None, 'eta', 'xi')
- inner_vel_new: float32 [3, 36, 1200], P(None, 'eta', 'xi')
- inner_acc_new: float32 [3, 36, 1200], P(None, 'eta', 'xi')
All inputs are finite; a program needn't handle non-finite values.
Results may differ from a plain program's by a relative error of at most 0.0001.
Values sent between devices are 32-bit elements; how exact they have to be, the bound alone decides.
No kernel may reach another device: no remote copies, remote signals or barrier semaphores. Data moves between devices by JAX's collectives and lax.ppermute only.
A program may use at most 64 MiB of HBM per device.

v0:
```python
import collections
import functools
import math

import jax
import jax.numpy as jnp
import numpy as np
from jax import lax
from jax.experimental import pallas as pl
from jax.experimental.pallas import tpu as pltpu
from jax.sharding import PartitionSpec as P


EX = 1
MANTLE_LAYERS = 2
INNER_LAYERS = 1
GROUPS = 6
ACROSS = 4 * EX + 1
RADIAL = 4 * MANTLE_LAYERS + 1
INNER_RADIAL = 4 * INNER_LAYERS + 1
LINES = ACROSS * GROUPS
WIDTH = LINES * RADIAL
INNER_WIDTH = LINES * INNER_RADIAL
COLUMN = GROUPS * RADIAL
NODES = LINES * 5 * MANTLE_LAYERS
PAD = 384
INNER_PAD = 256
ENTRIES = 128
BLOCK = 8
RUN_ROWS = 3
RUN_POINTS = 5
RUNS = 2
CLASS = 24
time_step = 0.1

MM, CF, CM, IF, IM, CW, FIELDS = 3, 4, 5, 6, 9, 10, 11
PAIRS = 6
CHANNELS = 10 * INNER_RADIAL + 6 * (RADIAL - INNER_RADIAL) + 2


def channel(r, f):
    if f == CW:
        return {0: CHANNELS - 2, RADIAL - 1: CHANNELS - 1}.get(r)
    if r < INNER_RADIAL:
        return 10 * r + f
    return 10 * INNER_RADIAL + 6 * (r - INNER_RADIAL) + f if f < IF else None


def runs_of(r):
    out = [(0, IF if r >= INNER_RADIAL else CW, channel(r, 0))]
    if channel(r, CW) is not None:
        out.append((CW, FIELDS, channel(r, CW)))
    return out


def gll_tables():
    radical = math.sqrt(3.0 / 7.0)
    points = np.array([-1.0, -radical, 0.0, radical, 1.0])
    weights = np.array([0.1, 49.0 / 90.0, 32.0 / 45.0, 49.0 / 90.0, 0.1])
    products = np.array(
        [np.prod([points[a] - points[c] for c in range(5) if c != a]) for a in range(5)]
    )
    slopes = np.zeros((5, 5))
    for a in range(5):
        for b in range(5):
            if a == b:
                slopes[a, b] = np.sum([1.0 / (points[a] - points[c]) for c in range(5) if c != a])
            else:
                slopes[a, b] = products[a] / (products[b] * (points[a] - points[b]))
    return weights, slopes


def spread_table(count):
    spread = np.zeros((4 * count + 1, 5 * count))
    for element in range(count):
        for node in range(5):
            spread[4 * element + node, 5 * element + node] = 1.0
    return spread


def padded(table, width):
    return np.pad(table, ((0, 0), (0, width - table.shape[1])))


def lane_tables(layers, width):
    weights, slopes = gll_tables()
    spread = spread_table(layers)
    derive = np.kron(np.eye(layers), slopes.T)
    eye_k = np.eye(GROUPS)
    along_x = np.kron(slopes.T, np.kron(eye_k, spread))
    along_r = np.kron(np.eye(ACROSS), np.kron(eye_k, spread @ derive))
    plain = np.kron(np.eye(ACROSS), np.kron(eye_k, spread))
    node = np.kron(weights, np.kron(np.ones(GROUPS), np.tile(weights, layers)))
    lumped_r = spread @ np.tile(weights, layers)
    lumped = np.kron(weights, np.kron(np.ones(GROUPS), lumped_r))
    table = np.concatenate([padded(t, width) for t in (along_x, along_r, plain)], axis=1)
    return table.astype(np.float32), node.astype(np.float32), lumped.astype(np.float32)


def constants(rows_local):
    weights, slopes = gll_tables()
    count_y = (rows_local - 1) // 4
    ypad = -(-rows_local // 8) * 8
    table, node, lumped = lane_tables(MANTLE_LAYERS, PAD)
    inner_table, inner_node, inner_lumped = lane_tables(INNER_LAYERS, INNER_PAD)
    small = np.eye(RADIAL)[:INNER_RADIAL]
    spread = np.kron(np.eye(LINES), small)
    lumped_y = spread_table(count_y) @ np.tile(weights, count_y)
    lanes = np.zeros((8, PAD))
    lanes[0, :NODES] = node
    lanes[1, :WIDTH] = lumped
    lanes[2, :WIDTH] = np.kron(weights, np.ones(COLUMN))
    lanes[3, : INNER_WIDTH] = inner_node
    lanes[4, : INNER_WIDTH] = inner_lumped
    columns = np.zeros((ypad, 8))
    columns[:rows_local, 0] = lumped_y
    columns[:5, 1] = weights
    along_y = np.zeros((16, 8))
    along_y[:5, :5] = slopes
    along_y[8:13, :5] = slopes.T
    pick = np.zeros((RADIAL * 32, PAD))
    for r in range(RADIAL):
        for line in range(LINES):
            pick[r * 32 + line, line * RADIAL + r] = 1.0
    polar = np.zeros((PAIRS * 128, 256))
    for f in range(FIELDS):
        for k in (4, 5):
            for r in range(RADIAL):
                if channel(r, f) is not None:
                    polar[(f // 2) * 128 + (f % 2) * 64 + k * RADIAL + r, (k - 4) * 128 + channel(r, f)] = 1.0
    as_f32 = lambda t: np.asarray(t, np.float32)
    as_bf16 = lambda t: np.asarray(t, np.float32).astype(bf16)

    def split(t):
        rest = as_f32(t)
        out = []
        for _ in range(3):
            out.append(rest.astype(bf16))
            rest = rest - out[-1].astype(np.float32)
        return np.stack(out)

    return dict(
        table=split(table[:, : 2 * PAD]),
        plain=as_bf16(table[:, 2 * PAD :]),
        inner_table=split(inner_table[:, : 2 * INNER_PAD]),
        spread=as_bf16(padded(spread, PAD)),
        squeeze=as_bf16(np.pad(spread.T, ((0, PAD - WIDTH), (0, 0)))),
        lanes=as_f32(lanes),
        columns=as_f32(columns),
        along_y=as_f32(along_y),
        pick=as_bf16(pick),
        polar=as_bf16(polar),
        polar_back=as_bf16(polar.T),
    )


def exchange_tables(count_x, count_y, rows):
    reach_x, reach_y = ACROSS - 1, rows - 1
    side = count_x * reach_x
    ypad = -(-rows // 8) * 8

    def canonical(j, i, y, x, k):
        gy, gx = j * reach_y + y, i * reach_x + x
        if k < 4 and gx == side:
            k, gx = (k + 1) % 4, 0
        if k < 4 and gy == side:
            gx, gy = ((gx, 0), (side, gx), (side - gx, side), (0, side - gx))[k]
            k = 4
        elif k < 4 and gy == 0:
            gx, gy = ((gx, side), (side, side - gx), (side - gx, 0), (0, gx))[k]
            k = 5
        return k, gy, gx

    def swapped(source, target):
        sj, si, sy, sx, sk = source
        j, i, y, x, k = target
        if sj == j and sy == y:
            if (x, sx) == (reach_x, 0):
                if (si, sk) == (i + 1, k):
                    return True
                if i == count_x - 1 and si == 0 and k < 4 and sk == (k + 1) % 4:
                    return True
            if (x, sx) == (0, reach_x):
                if (si, sk) == (i - 1, k):
                    return True
                if i == 0 and si == count_x - 1 and k < 4 and sk == (k - 1) % 4:
                    return True
        if si == i and sx == x:
            if sk == k and (sj, sy, y) in ((j + 1, 0, reach_y), (j - 1, reach_y, 0)):
                return True
            if (j, y, sj, sy) == (0, 0, count_y - 1, reach_y) and (k, sk) in ((4, 0), (0, 5)):
                return True
            if (j, y, sj, sy) == (count_y - 1, reach_y, 0, 0) and (k, sk) in ((0, 4), (5, 0)):
                return True
        return False

    def row_of(y, x, k):
        if y == reach_y:
            return x * GROUPS + k
        if y == 0:
            return 32 + x * GROUPS + k
        return 64 + (k - 4) * 2 * ypad + (ypad if x else 0) + y

    copies = collections.defaultdict(list)
    for j in range(count_y):
        for i in range(count_x):
            for y in range(rows):
                for x in range(ACROSS):
                    if 0 < y < reach_y and 0 < x < reach_x:
                        continue
                    for k in range(GROUPS):
                        copies[canonical(j, i, y, x, k)].append((j, i, y, x, k))
    pairs = collections.defaultdict(list)
    for members in copies.values():
        for target in members:
            for source in members:
                if source != target and not swapped(source, target):
                    key = (source[1] * count_y + source[0], target[1] * count_y + target[0])
                    pairs[key].append((row_of(*source[2:]), row_of(*target[2:])))
    table = np.full((count_x * count_y, 8, ENTRIES), -1.0, np.float32)
    sent = collections.Counter()
    taken = collections.Counter()
    peers = count_x * count_y
    for (source, target), links in sorted(pairs.items()):
        assert len(links) <= RUNS * RUN_POINTS
        for slot, (row_from, row_to) in enumerate(sorted(links)):
            run, place = divmod(slot, RUN_POINTS)
            for device, peer, row, counts, base in (
                (source, target, row_from, sent, 0),
                (target, source, row_to, taken, 2),
            ):
                assert counts[device, place] < CLASS
                entry = place * CLASS + counts[device, place]
                counts[device, place] += 1
                table[device, base, entry] = run * peers + peer
                table[device, base + 1, entry] = row
    return table


bf16 = jnp.bfloat16


def parts_of(x):
    high = x.astype(bf16)
    rest = x - high.astype(jnp.float32)
    middle = rest.astype(bf16)
    return high, middle, (rest - middle.astype(jnp.float32)).astype(bf16)


def product(a, b, back=False):
    dims = (((1,), (1 if back else 0,)), ((), ()))
    return lax.dot_general(a, b, dims, preferred_element_type=jnp.float32)


def pick_right(x, chosen):
    count = x.shape[0]
    out = product(jnp.concatenate(parts_of(x), axis=0), chosen)
    return out[0:count] + out[count : 2 * count] + out[2 * count : 3 * count]


def pick_left(chosen, x):
    width = x.shape[1]
    out = product(chosen, jnp.concatenate(parts_of(x), axis=1))
    return out[:, 0:width] + out[:, width : 2 * width] + out[:, 2 * width : 3 * width]


def times(x, table, lanes, back=False):
    count = x.shape[0]
    high, middle, low = parts_of(x)
    out = product(jnp.concatenate([high, middle, low], axis=0), table[0, :, lanes], back)
    total = out[0:count] + (out[count : 2 * count] + out[2 * count : 3 * count])
    out = product(jnp.concatenate([high, middle], axis=0), table[1, :, lanes], back)
    total = total + (out[0:count] + out[count : 2 * count])
    return total + product(high, table[2, :, lanes], back)


def turn_lanes(x, shift):
    shift = shift % x.shape[1]
    return pltpu.roll(x, shift, axis=1) if shift else x


def chosen_by(condition):
    return jnp.where(condition, 1.0, 0.0).astype(bf16)


def iota(shape, axis):
    return lax.broadcasted_iota(jnp.int32, shape, axis)


def put(ref, row, block):
    for t in range(ref.shape[0]):
        width = min(128, block.shape[1] - 128 * t)
        ref[t, row : row + block.shape[0], 0:width] = block[:, 128 * t : 128 * t + width]


def take(ref, c, first, count):
    tiles = [ref[t, pl.ds(4 * first + c, count, stride=4), :] for t in range(ref.shape[0])]
    return jnp.concatenate(tiles, axis=1)


def scatter(ref, c, block):
    for t in range(ref.shape[0]):
        ref[t, pl.ds(c, block.shape[0], stride=4), :] = block[:, 128 * t : 128 * t + 128]


def own_table(table_ref, count_y):
    return table_ref[lax.axis_index("xi") * count_y + lax.axis_index("eta")]


def force_kernel(
    rows,
    count_x,
    count_y,
    disp,
    vel,
    acc,
    metric,
    moduli,
    rho,
    pot,
    rate,
    accel,
    core_metric,
    kappa,
    core_rho,
    inner_disp,
    inner_vel,
    inner_acc,
    inner_metric,
    inner_moduli,
    inner_rho,
    table_ref,
    forward,
    plain_lanes,
    inner_forward,
    spread,
    lanes,
    columns,
    along_y,
    pick,
    polar,
    disp_next,
    pot_next,
    inner_next,
    fields,
    send_xa,
    send_xb,
    send_ya,
    send_yb,
    send_all,
    wide,
    narrow,
    inner_rows,
    flux,
    inner_flux,
    wide_u,
    edges,
    rows_t,
    points,
    moved,
    scale,
    lame,
    core_scale,
    inner_moved,
    inner_scale,
    inner_lame,
    stack,
    shifted,
):
    ne = (rows - 1) // 4
    ypad = edges.shape[0] // 2
    half = 0.5 * time_step * time_step
    for y in range(rows):
        block = disp[y] + time_step * vel[y] + half * acc[y]
        disp_next[y] = block
        put(moved, 4 * y, block)
        put(scale, 4 * y, metric[y])
        put(lame, 4 * y, moduli[y])
        put(core_scale, 4 * y, core_metric[y])
        block = inner_disp[y] + time_step * inner_vel[y] + half * inner_acc[y]
        inner_next[y] = block
        put(inner_moved, 4 * y, block)
        put(inner_scale, 4 * y, inner_metric[y])
        put(inner_lame, 4 * y, inner_moduli[y])

    def part(ref, c, first=0, count=rows):
        width = WIDTH if ref.shape[0] * 128 == PAD else INNER_WIDTH
        return take(ref, c, first, count)[:, 0:width]

    pot_next[...] = pot[...] + time_step * rate[...] + half * accel[...]

    slope = along_y[0:5, 0:5]
    slope_back = along_y[8:13, 0:5]

    def along(matrix, block):
        total = matrix[:, 0:1] * block[0:1, :]
        for b in range(1, 5):
            total = total + matrix[:, b : b + 1] * block[b : b + 1, :]
        return total

    wide[...] = jnp.zeros(wide.shape, jnp.float32)
    narrow[...] = jnp.zeros(narrow.shape, jnp.float32)
    inner_rows[...] = jnp.zeros(inner_rows.shape, jnp.float32)
    flux[...] = jnp.zeros(flux.shape, jnp.float32)
    inner_flux[...] = jnp.zeros(inner_flux.shape, jnp.float32)
    stack[...] = jnp.zeros(stack.shape, jnp.float32)
    fields[...] = jnp.zeros(fields.shape, jnp.float32)

    def slot(f, e):
        return (f * ne + e) * 8

    extras = [(scale, c) for c in range(3)] + [(lame, c) for c in range(2)] + [(core_scale, c) for c in range(3)]
    for e in range(ne):
        for f in range(4):
            block = part(moved, f, 4 * e, 5) if f < 3 else pot_next[4 * e : 4 * e + 5, :]
            wide[slot(f, e) : slot(f, e) + 5, :] = block
            narrow[slot(f, e) : slot(f, e) + 5, :] = along(slope, block)
        for f, (ref, c) in enumerate(extras):
            narrow[slot(4 + f, e) : slot(4 + f, e) + 5, :] = part(ref, c, 4 * e, 5)
        narrow[slot(12, e) : slot(12, e) + 5, :] = core_rho[4 * e : 4 * e + 5, :]
        for f in range(3):
            inner_rows[slot(f, e) : slot(f, e) + 5, :] = part(inner_moved, f, 4 * e, 5)
    whole = slice(None)
    slopes_xr = times(wide[...], forward, whole)
    copies = pick_right(narrow[...], plain_lanes[...])
    inner_xr = times(inner_rows[...], inner_forward, whole)

    def elastic(g, lam, mu, sy, sx, sr, jw):
        scaled = [[sy[i] * g[0], sx[i] * g[1], sr[i] * g[2]] for i in range(3)]
        trace = lam * (scaled[0][0] + scaled[1][1] + scaled[2][2])
        out = [[None] * 3 for _ in range(3)]
        weighted = [jw * g[m] for m in range(3)]
        for i in range(3):
            for m in range(3):
                if i == m:
                    stress = 2.0 * mu * scaled[i][i] + trace
                else:
                    stress = mu * (scaled[i][m] + scaled[m][i])
                out[i][m] = stress * weighted[m]
        return out

    row_weight = columns[0:5, 1:2]
    valid = (iota((5, PAD), 1) < NODES) & (iota((5, PAD), 0) < 5)
    for e in range(ne):
        def plain(f):
            return copies[slot(f, e) : slot(f, e) + 5, :]

        def x_of(f):
            return slopes_xr[slot(f, e) : slot(f, e) + 5, 0:PAD]

        def r_of(f):
            return slopes_xr[slot(f, e) : slot(f, e) + 5, PAD : 2 * PAD]

        node = row_weight * lanes[0:1, :]
        g = [jnp.where(valid, plain(4 + m), 1.0) for m in range(3)]
        q = elastic(
            g,
            plain(7),
            plain(8),
            [plain(f) for f in range(3)],
            [x_of(f) for f in range(3)],
            [r_of(f) for f in range(3)],
            node / (g[0] * g[1] * g[2]),
        )
        g = [jnp.where(valid, plain(9 + m), 1.0) for m in range(3)]
        volume = node / (g[0] * g[1] * g[2] * jnp.where(valid, plain(12), 1.0))
        q.append(
            [
                volume * g[0] * g[0] * plain(3),
                volume * g[1] * g[1] * x_of(3),
                volume * g[2] * g[2] * r_of(3),
            ]
        )
        for f in range(4):
            at = slot(f, e)
            flux[at : at + 5, 0:PAD] = q[f][1]
            flux[at : at + 5, PAD : 2 * PAD] = q[f][2]
            flux[at : at + 5, 2 * PAD : 3 * PAD] = along(slope_back, q[f][0])

        def inner_x(f):
            return inner_xr[slot(f, e) : slot(f, e) + 5, 0:INNER_WIDTH]

        def inner_r(f):
            return inner_xr[slot(f, e) : slot(f, e) + 5, INNER_PAD : INNER_PAD + INNER_WIDTH]

        g = [part(inner_scale, m, 4 * e, 5) for m in range(3)]
        node = row_weight * lanes[3:4, 0:INNER_WIDTH]
        q = elastic(
            g,
            part(inner_lame, 0, 4 * e, 5),
            part(inner_lame, 1, 4 * e, 5),
            [along(slope, inner_rows[slot(f, e) : slot(f, e) + 5, :]) for f in range(3)],
            [inner_x(f) for f in range(3)],
            [inner_r(f) for f in range(3)],
            node / (g[0] * g[1] * g[2]),
        )
        for f in range(3):
            at = slot(f, e)
            inner_flux[at : at + 5, 0:INNER_WIDTH] = q[f][1]
            inner_flux[at : at + 5, INNER_PAD : INNER_PAD + INNER_WIDTH] = q[f][2]
            inner_flux[at : at + 5, 2 * INNER_PAD : 2 * INNER_PAD + INNER_WIDTH] = along(slope_back, q[f][0])

    back = times(flux[:, 0 : 2 * PAD], forward, whole, back=True)
    own_y = flux[:, 2 * PAD : 3 * PAD]
    count = own_y.shape[0]
    out = product(jnp.concatenate(parts_of(own_y), axis=0), plain_lanes[...], back=True)
    back = back + (out[0:count] + out[count : 2 * count] + out[2 * count : 3 * count])
    count = 3 * ne * 8
    stack[0:count, :] = (
        times(inner_flux[:, 0 : 2 * INNER_PAD], inner_forward, whole, back=True)
        + inner_flux[:, 2 * INNER_PAD : 2 * INNER_PAD + INNER_WIDTH]
    )
    lumped_y = columns[0:rows, 0:1]
    stack[count : count + rows, :] = inner_rho[...] * (
        lumped_y * lanes[4:5, 0:INNER_WIDTH] / (part(inner_scale, 0) * part(inner_scale, 1) * part(inner_scale, 2))
    )
    stack[count + ypad : count + ypad + rows, :] = part(inner_moved, 2)
    spreads = pick_right(stack[...], spread[...])
    inner_forces = spreads[0:count, 0:WIDTH]
    for e in range(ne):
        here = slice(4 * e, 4 * e + 5)
        for f in range(3):
            fields[f, here, 0:WIDTH] = fields[f, here, 0:WIDTH] - back[slot(f, e) : slot(f, e) + 5, :]
            fields[IF + f, here, 0:WIDTH] = fields[IF + f, here, 0:WIDTH] - inner_forces[slot(f, e) : slot(f, e) + 5, :]
        fields[CF, here, 0:WIDTH] = fields[CF, here, 0:WIDTH] - back[slot(3, e) : slot(3, e) + 5, :]

    lumped = lumped_y * lanes[1:2, 0:WIDTH]
    fields[MM, 0:rows, 0:WIDTH] = rho[...] * (lumped / (part(scale, 0) * part(scale, 1) * part(scale, 2)))
    fields[CM, 0:rows, 0:WIDTH] = lumped / (part(core_scale, 0) * part(core_scale, 1) * part(core_scale, 2)) / kappa[...]
    fields[IM, 0:rows, :] = spreads[count : count + rows]
    radial = lax.rem(iota((rows, WIDTH), 1), RADIAL)
    face = lumped_y * lanes[2:3, 0:WIDTH] / (part(core_scale, 0) * part(core_scale, 1))
    face = jnp.where((radial == 0) | (radial == RADIAL - 1), face, 0.0)
    fields[CW, 0:rows, 0:WIDTH] = face
    wide_u[...] = jnp.zeros(wide_u.shape, jnp.float32)
    wide_u[0:rows, 0:WIDTH] = part(moved, 2)
    above = pltpu.roll(wide_u[...], RADIAL - 1, axis=1)
    below = pltpu.roll(spreads[count + ypad : count + 2 * ypad], PAD - (INNER_RADIAL - 1), axis=1)
    radial = lax.rem(iota((ypad, PAD), 1), RADIAL)
    jump = jnp.where(radial == RADIAL - 1, above, jnp.where(radial == 0, -below, 0.0))
    fields[CF] = fields[CF] + fields[CW] * jump

    low = iota((ypad, 128), 1) < 64
    for p in range(PAIRS):
        left = fields[2 * p]
        right = fields[2 * p + 1] if 2 * p + 1 < FIELDS else jnp.zeros_like(left)
        edges[0:ypad, p * 128 : p * 128 + 128] = jnp.where(low, left[:, 0:128], pltpu.roll(right[:, 0:128], 64, axis=1))
        edges[ypad : 2 * ypad, p * 128 : p * 128 + 128] = jnp.where(
            low,
            pltpu.roll(left, PAD - (WIDTH - COLUMN), axis=1)[:, 0:128],
            pltpu.roll(right, PAD + 64 - (WIDTH - COLUMN), axis=1)[:, 0:128],
        )
    even_x = lax.rem(lax.axis_index("xi"), 2) == 0
    even_y = lax.rem(lax.axis_index("eta"), 2) == 0
    for p in range(PAIRS):
        first = edges[0:rows, p * 128 : p * 128 + 128]
        last = edges[ypad : ypad + rows, p * 128 : p * 128 + 128]
        send_xa[p * rows : (p + 1) * rows, :] = jnp.where(even_x, last, first)
        send_xb[p * rows : (p + 1) * rows, :] = jnp.where(even_x, first, last)
    rows_t[...] = jnp.zeros(rows_t.shape, jnp.float32)
    for f in range(FIELDS):
        rows_t[f : f + 1, :] = fields[f, rows - 1 : rows, :]
        rows_t[64 + f : 65 + f, :] = fields[f, 0:1, :]
    top = rows_t[0:16, :]
    bottom = rows_t[64:80, :]
    send_ya[...] = jnp.where(even_y, top, bottom)
    send_yb[...] = jnp.where(even_y, bottom, top)

    for at, block in ((0, top), (64, bottom)):
        for n, piece in enumerate(parts_of(block)):
            rows_t[at + 16 * n : at + 16 * n + 16, :] = piece.astype(jnp.float32)
    by_line = product(pick[...], rows_t[...].astype(bf16), back=True)
    by_line = by_line + (pltpu.roll(by_line, 128 - 16, axis=1) + pltpu.roll(by_line, 128 - 32, axis=1))
    lane = iota((32, 128), 1)
    top_points = jnp.zeros((32, 128), jnp.float32)
    bottom_points = jnp.zeros((32, 128), jnp.float32)
    for r in range(RADIAL):
        block = by_line[32 * r : 32 * r + 32, :]
        for first, end, at in runs_of(r):
            upper = jnp.where((lane >= first) & (lane < end), block, 0.0)
            lower = jnp.where((lane >= 64 + first) & (lane < 64 + end), block, 0.0)
            top_points = top_points + turn_lanes(upper, at - first)
            bottom_points = bottom_points + turn_lanes(lower, at - first - 64)
    points[0:32, :] = top_points
    points[32:64, :] = bottom_points
    caps = pick_right(edges[...], polar[...])
    points[64 : 64 + 2 * ypad, :] = caps[:, 0:128]
    points[64 + 2 * ypad : 64 + 4 * ypad, :] = caps[:, 128:256]

    own = own_table(table_ref, count_y)
    turned = jnp.transpose(own)
    count = points.shape[0]
    chosen = chosen_by(turned[:, 1:2] == iota((ENTRIES, count), 1).astype(jnp.float32))
    chosen = pick_left(chosen, points[...])
    shifted[...] = jnp.zeros(shifted.shape, jnp.float32)
    lane = iota((CLASS, 128), 1)
    for place in range(RUN_POINTS):
        tile, shift = divmod(place * CHANNELS, 128)
        here = slice(place * CLASS, (place + 1) * CLASS)
        block = turn_lanes(chosen[here], shift)
        shifted[here, tile * 128 : tile * 128 + 128] = jnp.where(lane >= shift, block, 0.0)
        if shift + CHANNELS > 128:
            shifted[here, tile * 128 + 128 : tile * 128 + 256] = jnp.where(lane < shift, block, 0.0)
    peers = count_x * count_y
    number = iota((RUNS * peers, ENTRIES), 0).astype(jnp.float32)
    placed = pick_left(chosen_by(own[0:1, :] == number), shifted[...])
    for row in range(BLOCK):
        run, tile = divmod(row, RUN_ROWS)
        if run < RUNS:
            block = placed[run * peers : (run + 1) * peers, tile * 128 : tile * 128 + 128]
        else:
            block = jnp.zeros((peers, 128), jnp.float32)
        send_all[pl.ds(row, peers, stride=BLOCK), :] = block


def close_kernel(
    rows,
    count_x,
    count_y,
    got_xa,
    got_xb,
    got_ya,
    got_yb,
    got_all,
    fields,
    vel,
    acc,
    rate,
    accel,
    inner_vel,
    inner_acc,
    table_ref,
    pick,
    polar_back,
    squeeze,
    vel_next,
    acc_next,
    rate_next,
    accel_next,
    inner_vel_next,
    inner_acc_next,
    total,
    by_line,
    caps,
    narrow,
    wide,
    runs,
    arrived,
):
    ypad = total.shape[1]
    narrow[...] = jnp.zeros(narrow.shape, jnp.float32)
    own = own_table(table_ref, count_y)
    turned = jnp.transpose(own)
    peers = count_x * count_y
    for run in range(RUNS):
        for tile in range(RUN_ROWS):
            runs[run * peers : (run + 1) * peers, tile * 128 : tile * 128 + 128] = got_all[
                pl.ds(run * RUN_ROWS + tile, peers, stride=BLOCK), :
            ]
    number = iota((ENTRIES, RUNS * peers), 1).astype(jnp.float32)
    shifted = pick_left(chosen_by(turned[:, 2:3] == number), runs[...])
    lane = iota((CLASS, 128), 1)
    arrived[...] = jnp.zeros(arrived.shape, jnp.float32)
    for place in range(RUN_POINTS):
        tile, shift = divmod(place * CHANNELS, 128)
        here = slice(place * CLASS, (place + 1) * CLASS)
        block = shifted[here, tile * 128 : tile * 128 + 128]
        if shift + CHANNELS > 128:
            block = jnp.where(lane >= shift, block, shifted[here, tile * 128 + 128 : tile * 128 + 256])
        arrived[here, :] = jnp.where(lane < CHANNELS, turn_lanes(block, -shift), 0.0)
    count = 64 + 4 * ypad
    points = pick_left(chosen_by(own[3:4, :] == iota((count, ENTRIES), 0).astype(jnp.float32)), arrived[...])
    lane = iota((32, 128), 1)
    upper = points[0:32]
    lower = points[32:64]
    for r in range(RADIAL):
        block = jnp.zeros((32, 128), jnp.float32)
        for first, end, at in runs_of(r):
            high = turn_lanes(upper, first - at)
            low = turn_lanes(lower, 64 + first - at)
            block = jnp.where((lane >= first) & (lane < end), high, block)
            block = jnp.where((lane >= 64 + first) & (lane < 64 + end), low, block)
        high, middle, last = (piece.astype(jnp.float32) for piece in parts_of(block))
        by_line[32 * r : 32 * r + 32, :] = (
            high + pltpu.roll(middle, 16, axis=1) + pltpu.roll(last, 32, axis=1)
        )
    lines = lax.dot_general(
        by_line[...].astype(bf16), pick[...], (((0,), (0,)), ((), ())), preferred_element_type=jnp.float32
    )
    lines_top = lines[0:16] + (lines[16:32] + lines[32:48])
    lines_bottom = lines[64:80] + (lines[80:96] + lines[96:112])
    caps[:, 0:128] = points[64 : 64 + 2 * ypad]
    caps[:, 128:256] = points[64 + 2 * ypad : 64 + 4 * ypad]
    columns = pick_right(caps[...], polar_back[...])

    xi = lax.axis_index("xi")
    eta = lax.axis_index("eta")
    even_x = lax.rem(xi, 2) == 0
    even_y = lax.rem(eta, 2) == 0
    lane = iota((16, PAD), 1)
    group = lax.rem(lane // RADIAL, GROUPS)
    used = lane < WIDTH
    ya = got_ya[...]
    yb = got_yb[...]
    from_above = jnp.where(even_y, ya, yb)
    from_below = jnp.where(even_y, yb, ya)
    four, five = 4 * RADIAL, 5 * RADIAL
    seam_top = jnp.where(
        group == 0,
        pltpu.roll(from_above, PAD - four, axis=1),
        jnp.where(group == 5, pltpu.roll(from_above, five, axis=1), 0.0),
    )
    seam_bottom = jnp.where(
        group == 4,
        pltpu.roll(from_below, four, axis=1),
        jnp.where(group == 0, pltpu.roll(from_below, PAD - five, axis=1), 0.0),
    )
    add_top = jnp.where(eta == count_y - 1, seam_top, from_above) + lines_top
    add_bottom = jnp.where(eta == 0, seam_bottom, from_below) + lines_bottom
    add_top = jnp.where(used, add_top, 0.0)
    add_bottom = jnp.where(used, add_bottom, 0.0)
    total[...] = fields[...]
    lane = iota((rows, 128), 1)
    inside = lax.rem(lane, 64)
    equator = inside < 4 * RADIAL
    keep = inside < COLUMN
    low = lane < 64
    last_x = xi == count_x - 1
    for p in range(PAIRS):
        xa = got_xa[p * rows : (p + 1) * rows, :]
        xb = got_xb[p * rows : (p + 1) * rows, :]
        from_right = jnp.where(even_x, xa, xb)
        from_left = jnp.where(even_x, xb, xa)
        up = jnp.where(
            inside < 3 * RADIAL,
            pltpu.roll(from_right, 128 - RADIAL, axis=1),
            pltpu.roll(from_right, 3 * RADIAL, axis=1),
        )
        down = jnp.where(
            inside < RADIAL,
            pltpu.roll(from_left, 128 - 3 * RADIAL, axis=1),
            pltpu.roll(from_left, RADIAL, axis=1),
        )
        from_right = jnp.where(last_x, jnp.where(equator, up, 0.0), from_right)
        from_left = jnp.where(xi == 0, jnp.where(equator, down, 0.0), from_left)
        at = slice(p * 128, p * 128 + 128)
        from_left = jnp.where(keep, from_left + columns[0:rows, at], 0.0)
        from_right = jnp.where(keep, from_right + columns[ypad : ypad + rows, at], 0.0)
        zero = jnp.zeros((rows, PAD - 128), jnp.float32)
        for h in range(2):
            f = 2 * p + h
            if f >= FIELDS:
                continue
            mine = low if h == 0 else ~low
            left = jnp.where(mine, from_left, 0.0)
            right = jnp.where(mine, from_right, 0.0)
            if h:
                left = pltpu.roll(left, 64, axis=1)
            total[f, 0:rows, 0:128] = total[f, 0:rows, 0:128] + left
            right = jnp.concatenate([right, zero], axis=1)
            right = pltpu.roll(right, WIDTH - COLUMN - 64 * h, axis=1)
            total[f, 0:rows, :] = total[f, 0:rows, :] + right
    for f in range(FIELDS):
        total[f, rows - 1 : rows, :] = total[f, rows - 1 : rows, :] + add_top[f : f + 1, :]
        total[f, 0:1, :] = total[f, 0:1, :] + add_bottom[f : f + 1, :]

    half = 0.5 * time_step
    lane = iota((ypad, PAD), 1)
    radial = lax.rem(lane, RADIAL)
    inside = (lane < WIDTH) & (iota((ypad, PAD), 0) < rows)
    core = total[CF] / jnp.where(inside, total[CM], 1.0)
    accel_next[...] = core[0:rows, 0:WIDTH]
    rate_next[...] = rate[...] + half * (accel[...] + core[0:rows, 0:WIDTH])
    push = total[CW] * core
    top = jnp.where(radial == 0, pltpu.roll(push, PAD - (RADIAL - 1), axis=1), 0.0)
    bottom = jnp.where(radial == INNER_RADIAL - 1, pltpu.roll(push, INNER_RADIAL - 1, axis=1), 0.0)
    mass = jnp.where(inside, total[MM], 1.0)
    inner_mass = jnp.where(inside & (radial < INNER_RADIAL), total[IM], 1.0)
    for f in range(3):
        force = total[f] + top if f == 2 else total[f]
        result = (force / mass)[0:rows]
        scatter(wide, f, result)
        force = total[IF + f] - bottom if f == 2 else total[IF + f]
        scatter(narrow, f, (force / inner_mass)[0:rows])
    squeezed = pick_right(jnp.concatenate([narrow[t] for t in range(PAD // 128)], axis=1), squeeze[...])
    for y in range(rows):
        result = jnp.concatenate([wide[t, 4 * y : 4 * y + 3, :] for t in range(PAD // 128)], axis=1)[:, 0:WIDTH]
        acc_next[y] = result
        vel_next[y] = vel[y] + half * (acc[y] + result)
        result = squeezed[4 * y : 4 * y + 3, :]
        inner_acc_next[y] = result
        inner_vel_next[y] = inner_vel[y] + half * (inner_acc[y] + result)


def shards(
    count_x,
    count_y,
    mantle_disp,
    mantle_vel,
    mantle_acc,
    mantle_metric,
    mantle_moduli,
    mantle_rho,
    core_pot,
    core_rate,
    core_accel,
    core_metric,
    core_kappa,
    core_rho,
    inner_disp,
    inner_vel,
    inner_acc,
    inner_metric,
    inner_moduli,
    inner_rho,
):
    rows = mantle_disp.shape[1]
    turn = lambda a: jnp.transpose(a, (1, 0, 2))
    mantle_disp, mantle_vel, mantle_acc = turn(mantle_disp), turn(mantle_vel), turn(mantle_acc)
    mantle_metric, mantle_moduli, core_metric = turn(mantle_metric), turn(mantle_moduli), turn(core_metric)
    inner_disp, inner_vel, inner_acc = turn(inner_disp), turn(inner_vel), turn(inner_acc)
    inner_metric, inner_moduli = turn(inner_metric), turn(inner_moduli)
    ne = (rows - 1) // 4
    ypad = -(-rows // 8) * 8
    tables = {name: jnp.asarray(value) for name, value in constants(rows).items()}
    table = jnp.asarray(exchange_tables(count_x, count_y, rows))
    f32 = jnp.float32
    like = lambda a: jax.ShapeDtypeStruct(a.shape, f32)
    shape = lambda *s: jax.ShapeDtypeStruct(s, f32)
    devices = count_x * count_y
    edge = -(-PAIRS * rows // 8) * 8
    (mantle_next, core_next, inner_next, fields, xa, xb, ya, yb, everyone) = pl.pallas_call(
        functools.partial(force_kernel, rows, count_x, count_y),
        out_shape=[
            like(mantle_disp),
            like(core_pot),
            like(inner_disp),
            shape(FIELDS, ypad, PAD),
            shape(edge, 128),
            shape(edge, 128),
            shape(16, PAD),
            shape(16, PAD),
            shape(devices * BLOCK, 128),
        ],
        scratch_shapes=[
            pltpu.VMEM((4 * ne * 8, WIDTH), f32),
            pltpu.VMEM((13 * ne * 8, WIDTH), f32),
            pltpu.VMEM((3 * ne * 8, INNER_WIDTH), f32),
            pltpu.VMEM((4 * ne * 8, 3 * PAD), f32),
            pltpu.VMEM((3 * ne * 8, 3 * INNER_PAD), f32),
            pltpu.VMEM((ypad, PAD), f32),
            pltpu.VMEM((2 * ypad, PAIRS * 128), f32),
            pltpu.VMEM((128, PAD), f32),
            pltpu.VMEM((64 + 4 * ypad, 128), f32),
        ]
        + [pltpu.VMEM((PAD // 128, 4 * rows, 128), f32)] * 4
        + [pltpu.VMEM((INNER_PAD // 128, 4 * rows, 128), f32)] * 3
        + [pltpu.VMEM((3 * ne * 8 + 2 * ypad, INNER_WIDTH), f32)]
        + [pltpu.VMEM((ENTRIES, RUN_ROWS * 128), f32)],
        name="forces",
    )(
        mantle_disp,
        mantle_vel,
        mantle_acc,
        mantle_metric,
        mantle_moduli,
        mantle_rho,
        core_pot,
        core_rate,
        core_accel,
        core_metric,
        core_kappa,
        core_rho,
        inner_disp,
        inner_vel,
        inner_acc,
        inner_metric,
        inner_moduli,
        inner_rho,
        table,
        tables["table"],
        tables["plain"],
        tables["inner_table"],
        tables["spread"],
        tables["lanes"],
        tables["columns"],
        tables["along_y"],
        tables["pick"],
        tables["polar"],
    )
    everyone = lax.all_to_all(everyone, ("xi", "eta"), 0, 0, tiled=True)
    near = [(i, i ^ 1) for i in range(count_x)]
    far = [(i, (i - 1 if i % 2 == 0 else i + 1) % count_x) for i in range(count_x)]
    xa = lax.ppermute(xa, "xi", near)
    xb = lax.ppermute(xb, "xi", far)
    near = [(j, j ^ 1) for j in range(count_y)]
    far = [(j, (j - 1 if j % 2 == 0 else j + 1) % count_y) for j in range(count_y)]
    ya = lax.ppermute(ya, "eta", near)
    yb = lax.ppermute(yb, "eta", far)
    (mantle_vel_next, mantle_acc_next, core_rate_next, core_acc_next, inner_vel_next, inner_acc_next) = pl.pallas_call(
        functools.partial(close_kernel, rows, count_x, count_y),
        out_shape=[
            like(mantle_vel),
            like(mantle_acc),
            like(core_rate),
            like(core_accel),
            like(inner_vel),
            like(inner_acc),
        ],
        scratch_shapes=[
            pltpu.VMEM((FIELDS, ypad, PAD), f32),
            pltpu.VMEM((RADIAL * 32, 128), f32),
            pltpu.VMEM((2 * ypad, 256), f32),
            pltpu.VMEM((PAD // 128, -(-4 * rows // 16) * 16, 128), f32),
            pltpu.VMEM((PAD // 128, 4 * rows, 128), f32),
            pltpu.VMEM((RUNS * devices, RUN_ROWS * 128), f32),
            pltpu.VMEM((ENTRIES, 128), f32),
        ],
        compiler_params=pltpu.CompilerParams(vmem_limit_bytes=(8 << 20) + devices * (48 << 10)),
        name="close",
    )(
        xa,
        xb,
        ya,
        yb,
        everyone,
        fields,
        mantle_vel,
        mantle_acc,
        core_rate,
        core_accel,
        inner_vel,
        inner_acc,
        table,
        tables["pick"],
        tables["polar_back"],
        tables["squeeze"],
    )
    return (
        turn(mantle_next),
        turn(mantle_vel_next),
        turn(mantle_acc_next),
        core_next,
        core_rate_next,
        core_acc_next,
        turn(inner_next),
        turn(inner_vel_next),
        turn(inner_acc_next),
    )


def solution(mesh):
    count_x, count_y = mesh.shape["xi"], mesh.shape["eta"]
    assert count_x % 2 == 0 and count_y % 2 == 0
    assert (count_x * count_y) % 8 == 0
    vector, scalar = P(None, "eta", "xi"), P("eta", "xi")
    placed = (vector,) * 5 + (scalar,) * 4 + (vector,) + (scalar,) * 2 + (vector,) * 5 + (scalar,)
    return jax.shard_map(
        functools.partial(shards, count_x, count_y),
        mesh=mesh,
        in_specs=placed,
        out_specs=(vector,) * 3 + (scalar,) * 3 + (vector,) * 3,
        check_vma=False,
    )
```

profile of v0, /device:TPU:0, one launch (start us, length us, event | category | flops | bytes accessed | tf_op | source)
XLA Modules:
  0.0 27.4 jit_solution(4462385942630102389)
XLA Ops:
  0.6 0.0 copy-start
  0.7 0.0 copy-start.1
  0.7 0.0 copy-start.2
  0.7 0.0 copy-start.4
  0.7 0.0 copy-start.5
  0.7 0.0 copy-start.6
  0.7 0.0 copy-start.7
  0.7 0.0 copy-start.8
  0.7 0.0 copy-start.9
  0.7 0.0 copy-start.10
  0.8 5.8 %forces.1 = (f32[9,3,270]{2,1,0:T(4,128)}, f32[9,270]{1,0:T(8,128)}, f32[9,3,150]{2,1,0:T(4,128)}, f32[11,16,384]{2,1,0:T(8,128)}, f32[56,128]{1,0:T(8,128)}, /*...) custom-call(f32[9,3,270]{2,1,0:T(4,128)} %bitcast.29, f32[9,3,270]{2,1,0:T(4,128)} %bitcast.20, ...), custom_call_target="tpu_custom_call" | custom-call | tf_op jit(solution)/shard_map/forces/pallas_call | solution.py:832
  6.6 7.3 %all-to-all-start = ((f32[32,8,128]{2,1,0:T(8,128)}), f32[32,8,128]{2,1,0:T(8,128)S(1)}, u32[]{:S(2)}, u32[]{:S(2)}) async-start(f32[32,8,128]{2,1,0:T(8,128)} %bitcast.28), calls=%async_computation | async-start | bytes 262144 | tf_op jit(solution)/shard_map/all_to_all | solution.py:891
  13.9 0.3 %collective-permute-start = (f32[56,128]{1,0:T(8,128)}, f32[56,128]{1,0:T(8,128)S(1)}, u32[]{:S(2)}, u32[]{:S(2)}) collective-permute-start(f32[56,128]{1,0:T(8,128)} %get-tuple-element.25), channel_id=1, source_target_pairs={{0,4},{4,0},{8,12},{12,8},{16,20},{20,16},{24,28},{28,24},{1,5},{5... | collective-permute-start | bytes 86024 | tf_op jit(solution)/shard_map/ppermute | solution.py:894
  14.3 3.5 %collective-permute-start.1 = (f32[56,128]{1,0:T(8,128)}, f32[56,128]{1,0:T(8,128)S(1)}, u32[]{:S(2)}, u32[]{:S(2)}) collective-permute-start(f32[56,128]{1,0:T(8,128)} %get-tuple-element.26), channel_id=1, source_target_pairs={{0,28},{4,8},{8,4},{12,16},{16,12},{20,24},{24,20},{28,0},{1,29},{... | collective-permute-start | bytes 86024 | tf_op jit(solution)/shard_map/ppermute | solution.py:895
  17.7 1.5 %collective-permute-start.2 = (f32[16,384]{1,0:T(8,128)}, f32[16,384]{1,0:T(8,128)S(1)}, u32[]{:S(2)}, u32[]{:S(2)}) collective-permute-start(f32[16,384]{1,0:T(8,128)} %get-tuple-element.27), channel_id=1, source_target_pairs={{0,1},{1,0},{2,3},{3,2},{4,5},{5,4},{6,7},{7,6},{8,9},{9,8},{10,11... | collective-permute-start | bytes 73736 | tf_op jit(solution)/shard_map/ppermute | solution.py:898
  19.2 1.5 %collective-permute-start.3 = (f32[16,384]{1,0:T(8,128)}, f32[16,384]{1,0:T(8,128)S(1)}, u32[]{:S(2)}, u32[]{:S(2)}) collective-permute-start(f32[16,384]{1,0:T(8,128)} %get-tuple-element.28), channel_id=1, source_target_pairs={{0,3},{1,2},{2,1},{3,0},{4,7},{5,6},{6,5},{7,4},{8,11},{9,10},{10,... | collective-permute-start | bytes 73736 | tf_op jit(solution)/shard_map/ppermute | solution.py:899
  20.7 1.1 %collective-permute-done.2.got_ya = f32[16,384]{1,0:T(8,128)S(1)} collective-permute-done((f32[16,384]{1,0:T(8,128)}, f32[16,384]{1,0:T(8,128)S(1)}, u32[]{:S(2)}, u32[]{:S(2)}) %collective-permute-start.2) | collective-permute-done | bytes 24608 | tf_op jit(solution)/shard_map/ppermute | solution.py:898
  21.8 2.4 %collective-permute-done.3.got_yb = f32[16,384]{1,0:T(8,128)S(1)} collective-permute-done((f32[16,384]{1,0:T(8,128)}, f32[16,384]{1,0:T(8,128)S(1)}, u32[]{:S(2)}, u32[]{:S(2)}) %collective-permute-start.3) | collective-permute-done | bytes 24608 | tf_op jit(solution)/shard_map/ppermute | solution.py:899
  24.2 0.0 collective-permute-done.got_xa
  24.2 0.0 collective-permute-done.1.got_xb
  24.2 0.0 all-to-all-done
  24.2 0.0 copy-done
  24.3 0.9 %copy-done.3 = f32[11,16,384]{2,1,0:T(8,128)S(1)} copy-done((f32[11,16,384]{2,1,0:T(8,128)S(1)}, f32[11,16,384]{2,1,0:T(8,128)}, u32[]{:S(2)}) %copy-start.3) | copy-done | bytes 270360
  25.2 2.1 %close.1 = (f32[9,3,270]{2,1,0:T(4,128)}, f32[9,3,270]{2,1,0:T(4,128)}, f32[9,270]{1,0:T(8,128)}, f32[9,270]{1,0:T(8,128)}, f32[9,3,150]{2,1,0:T(4,128)}, /*index=5*/f32[9,3,150]{2,1,0:T(4,128)}) custom-call(f32[56,128]{1,0:T(8,128)S(1)} %collective-permute-done.got_xa, f32[56,128]{1,0:T(8,128)S(1)} %collective-permute-done.1.got_xb, ...), custom_call_target="tpu_custom_call" | custom-call | tf_op jit(solution)/shard_map/close/pallas_call | solution.py:900
  (10 shorter events, 0.0 us)
Async XLA Ops:
  0.6 23.5 %copy-start = (bf16[288,384]{1,0:T(8,128)(2,1)S(1)}, bf16[288,384]{1,0:T(8,128)(2,1)}, u32[]{:S(2)}) copy-start(bf16[288,384]{1,0:T(8,128)(2,1)} %constant.32.clone.pick) | copy-start | bytes 663556
  0.7 23.5 %copy-start.1 = (f32[32,8,128]{2,1,0:T(8,128)S(1)}, f32[32,8,128]{2,1,0:T(8,128)}, u32[]{:S(2)}) copy-start(f32[32,8,128]{2,1,0:T(8,128)} %constant.35.clone.table_ref) | copy-start | bytes 393220
  0.7 23.5 %copy-start.2 = (bf16[256,768]{1,0:T(8,128)(2,1)S(1)}, bf16[256,768]{1,0:T(8,128)(2,1)}, u32[]{:S(2)}) copy-start(bf16[256,768]{1,0:T(8,128)(2,1)} %constant.34.clone.polar_back) | copy-start | bytes 1179652
  0.7 23.5 %copy-start.4 = (f32[3,9,270]{2,0,1:T(4,128)S(1)}, f32[3,9,270]{2,0,1:T(4,128)}, u32[]{:S(2)}) copy-start(f32[3,9,270]{2,0,1:T(4,128)} %param.31) | copy-start | bytes 87484
  0.7 23.5 %copy-start.5 = (f32[3,9,270]{2,0,1:T(4,128)S(1)}, f32[3,9,270]{2,0,1:T(4,128)}, u32[]{:S(2)}) copy-start(f32[3,9,270]{2,0,1:T(4,128)} %param.32) | copy-start | bytes 87484
  0.7 23.5 %copy-start.6 = (bf16[384,150]{1,0:T(8,128)(2,1)S(1)}, bf16[384,150]{1,0:T(8,128)(2,1)}, u32[]{:S(2)}) copy-start(bf16[384,150]{1,0:T(8,128)(2,1)} %constant.28.clone.squeeze) | copy-start | bytes 345604
  0.7 23.5 %copy-start.7 = (f32[3,9,150]{2,0,1:T(4,128)S(1)}, f32[3,9,150]{2,0,1:T(4,128)}, u32[]{:S(2)}) copy-start(f32[3,9,150]{2,0,1:T(4,128)} %param.43) | copy-start | bytes 48604
  0.7 23.5 %copy-start.8 = (f32[3,9,150]{2,0,1:T(4,128)S(1)}, f32[3,9,150]{2,0,1:T(4,128)}, u32[]{:S(2)}) copy-start(f32[3,9,150]{2,0,1:T(4,128)} %param.44) | copy-start | bytes 48604
  0.7 23.5 %copy-start.9 = (f32[9,270]{1,0:T(8,128)S(1)}, f32[9,270]{1,0:T(8,128)}, u32[]{:S(2)}) copy-start(f32[9,270]{1,0:T(8,128)} %rate.3) | copy-start | bytes 29164
  0.7 23.5 %copy-start.10 = (f32[9,270]{1,0:T(8,128)S(1)}, f32[9,270]{1,0:T(8,128)}, u32[]{:S(2)}) copy-start(f32[9,270]{1,0:T(8,128)} %accel.3) | copy-start | bytes 29164
  6.6 17.6 %all-to-all-start = ((f32[32,8,128]{2,1,0:T(8,128)}), f32[32,8,128]{2,1,0:T(8,128)S(1)}, u32[]{:S(2)}, u32[]{:S(2)}) async-start(f32[32,8,128]{2,1,0:T(8,128)} %bitcast.28), calls=%async_computation | async-start | bytes 262144 | tf_op jit(solution)/shard_map/all_to_all | solution.py:891
  13.9 10.2 %collective-permute-start = (f32[56,128]{1,0:T(8,128)}, f32[56,128]{1,0:T(8,128)S(1)}, u32[]{:S(2)}, u32[]{:S(2)}) collective-permute-start(f32[56,128]{1,0:T(8,128)} %get-tuple-element.25), channel_id=1, source_target_pairs={{0,4},{4,0},{8,12},{12,8},{16,20},{20,16},{24,28},{28,24},{1,5},{5... | collective-permute-start | bytes 86024 | tf_op jit(solution)/shard_map/ppermute | solution.py:894
  14.3 9.9 %collective-permute-start.1 = (f32[56,128]{1,0:T(8,128)}, f32[56,128]{1,0:T(8,128)S(1)}, u32[]{:S(2)}, u32[]{:S(2)}) collective-permute-start(f32[56,128]{1,0:T(8,128)} %get-tuple-element.26), channel_id=1, source_target_pairs={{0,28},{4,8},{8,4},{12,16},{16,12},{20,24},{24,20},{28,0},{1,29},{... | collective-permute-start | bytes 86024 | tf_op jit(solution)/shard_map/ppermute | solution.py:895
  17.7 4.0 %collective-permute-start.2 = (f32[16,384]{1,0:T(8,128)}, f32[16,384]{1,0:T(8,128)S(1)}, u32[]{:S(2)}, u32[]{:S(2)}) collective-permute-start(f32[16,384]{1,0:T(8,128)} %get-tuple-element.27), channel_id=1, source_target_pairs={{0,1},{1,0},{2,3},{3,2},{4,5},{5,4},{6,7},{7,6},{8,9},{9,8},{10,11... | collective-permute-start | bytes 73736 | tf_op jit(solution)/shard_map/ppermute | solution.py:898
  19.2 4.9 %collective-permute-start.3 = (f32[16,384]{1,0:T(8,128)}, f32[16,384]{1,0:T(8,128)S(1)}, u32[]{:S(2)}, u32[]{:S(2)}) collective-permute-start(f32[16,384]{1,0:T(8,128)} %get-tuple-element.28), channel_id=1, source_target_pairs={{0,3},{1,2},{2,1},{3,0},{4,7},{5,6},{6,5},{7,4},{8,11},{9,10},{10,... | collective-permute-start | bytes 73736 | tf_op jit(solution)/shard_map/ppermute | solution.py:899
  24.3 1.0 %copy-start.3 = (f32[11,16,384]{2,1,0:T(8,128)S(1)}, f32[11,16,384]{2,1,0:T(8,128)}, u32[]{:S(2)}) copy-start(f32[11,16,384]{2,1,0:T(8,128)} %get-tuple-element.30.fields) | copy-start | bytes 811012
where the time goes:
time: 27.6 us; the launch traced here: 27.4 us
  starting transfers between devices  14.1 us (51%)
  Pallas kernels  7.98 us (29%)
  waiting for transfers between devices  3.46 us (13%)
  local copies, waits for them, and re-layouts  1 us (4%)
  between operations  0.83 us (3%)
    all_to_all x1, starting transfers between devices, shards(): everyone = lax.all_to_all(everyone, ('xi', 'eta'), 0, 0, tiled=True)  7.33 us
    pallas_call x1, Pallas kernels, shards(): pl.pallas_call(functools.partial(force_kernel, rows, count_x, count_y), o...  5.85 us
    ppermute x1, starting transfers between devices, shards(): xb = lax.ppermute(xb, 'xi', far)  3.48 us
    ppermute x1, waiting for transfers between devices, shards(): yb = lax.ppermute(yb, 'eta', far)  2.37 us
    pallas_call x1, Pallas kernels, shards(): pl.pallas_call(functools.partial(close_kernel, rows, count_x, count_y), o...  2.14 us
    ppermute x1, starting transfers between devices, shards(): ya = lax.ppermute(ya, 'eta', near)  1.48 us
    ppermute x1, starting transfers between devices, shards(): yb = lax.ppermute(yb, 'eta', far)  1.48 us
    ppermute x1, waiting for transfers between devices, shards(): ya = lax.ppermute(ya, 'eta', near)  1.09 us
  transfers between devices with their start and end apart: 5, of which 2 were waited for; matrix products, arithmetic and copies ran while one was open for 0% of the time, Pallas kernels for 0%

commit v1 on v0

--- a/solution.py
+++ b/solution.py
@@ -25,12 +25,14 @@
 NODES = LINES * 5 * MANTLE_LAYERS
 PAD = 384
 INNER_PAD = 256
+TILE = 256
 ENTRIES = 128
 BLOCK = 8
 RUN_ROWS = 3
 RUN_POINTS = 5
 RUNS = 2
 CLASS = 24
+WINDOW_GRANT = 8 << 20
 time_step = 0.1
 
 MM, CF, CM, IF, IM, CW, FIELDS = 3, 4, 5, 6, 9, 10, 11
@@ -93,8 +95,16 @@
     node = np.kron(weights, np.kron(np.ones(GROUPS), np.tile(weights, layers)))
     lumped_r = spread @ np.tile(weights, layers)
     lumped = np.kron(weights, np.kron(np.ones(GROUPS), lumped_r))
-    table = np.concatenate([padded(t, width) for t in (along_x, along_r, plain)], axis=1)
+    order = node_order(layers)
+    node = node[order]
+    table = np.concatenate([padded(t[:, order], width) for t in (along_x, along_r, plain)], axis=1)
     return table.astype(np.float32), node.astype(np.float32), lumped.astype(np.float32)
+
+
+def node_order(layers):
+    radial = [max(0, (r - 1) // 4) for r in range(4 * layers + 1)]
+    plain = [line * 5 * layers + 5 * e + r - 4 * e for line in range(LINES) for r, e in enumerate(radial)]
+    return plain + [line * 5 * layers + 5 * e for e in range(1, layers) for line in range(LINES)]
 
 
 def constants(rows_local):
@@ -141,7 +151,7 @@
 
     return dict(
         table=split(table[:, : 2 * PAD]),
-        plain=as_bf16(table[:, 2 * PAD :]),
+        plain=as_bf16(table[:, 2 * PAD + TILE :] * (np.arange(TILE, PAD) >= WIDTH)),
         inner_table=split(inner_table[:, : 2 * INNER_PAD]),
         spread=as_bf16(padded(spread, PAD)),
         squeeze=as_bf16(np.pad(spread.T, ((0, PAD - WIDTH), (0, 0)))),
@@ -339,9 +349,6 @@
     along_y,
     pick,
     polar,
-    disp_next,
-    pot_next,
-    inner_next,
     fields,
     send_xa,
     send_xb,
@@ -366,19 +373,19 @@
     inner_lame,
     stack,
     shifted,
+    copies,
+    pot_next,
 ):
     ne = (rows - 1) // 4
     ypad = edges.shape[0] // 2
     half = 0.5 * time_step * time_step
     for y in range(rows):
         block = disp[y] + time_step * vel[y] + half * acc[y]
-        disp_next[y] = block
         put(moved, 4 * y, block)
         put(scale, 4 * y, metric[y])
         put(lame, 4 * y, moduli[y])
         put(core_scale, 4 * y, core_metric[y])
         block = inner_disp[y] + time_step * inner_vel[y] + half * inner_acc[y]
-        inner_next[y] = block
         put(inner_moved, 4 * y, block)
         put(inner_scale, 4 * y, inner_metric[y])
         put(inner_lame, 4 * y, inner_moduli[y])
@@ -398,11 +405,9 @@
             total = total + matrix[:, b : b + 1] * block[b : b + 1, :]
         return total
 
-    wide[...] = jnp.zeros(wide.shape, jnp.float32)
-    narrow[...] = jnp.zeros(narrow.shape, jnp.float32)
-    inner_rows[...] = jnp.zeros(inner_rows.shape, jnp.float32)
-    flux[...] = jnp.zeros(flux.shape, jnp.float32)
-    inner_flux[...] = jnp.zeros(inner_flux.shape, jnp.float32)
+    narrow[:, TILE:PAD] = jnp.zeros((narrow.shape[0], PAD - TILE), jnp.float32)
+    for first in (0, INNER_PAD):
+        inner_flux[:, first + 128 : first + 256] = jnp.zeros((inner_flux.shape[0], 128), jnp.float32)
     stack[...] = jnp.zeros(stack.shape, jnp.float32)
     fields[...] = jnp.zeros(fields.shape, jnp.float32)
 
@@ -414,15 +419,15 @@
         for f in range(4):
             block = part(moved, f, 4 * e, 5) if f < 3 else pot_next[4 * e : 4 * e + 5, :]
             wide[slot(f, e) : slot(f, e) + 5, :] = block
-            narrow[slot(f, e) : slot(f, e) + 5, :] = along(slope, block)
+            narrow[slot(f, e) : slot(f, e) + 5, 0:WIDTH] = along(slope, block)
         for f, (ref, c) in enumerate(extras):
-            narrow[slot(4 + f, e) : slot(4 + f, e) + 5, :] = part(ref, c, 4 * e, 5)
-        narrow[slot(12, e) : slot(12, e) + 5, :] = core_rho[4 * e : 4 * e + 5, :]
+            narrow[slot(4 + f, e) : slot(4 + f, e) + 5, 0:WIDTH] = part(ref, c, 4 * e, 5)
+        narrow[slot(12, e) : slot(12, e) + 5, 0:WIDTH] = core_rho[4 * e : 4 * e + 5, :]
         for f in range(3):
             inner_rows[slot(f, e) : slot(f, e) + 5, :] = part(inner_moved, f, 4 * e, 5)
     whole = slice(None)
     slopes_xr = times(wide[...], forward, whole)
-    copies = pick_right(narrow[...], plain_lanes[...])
+    copies[...] = narrow[:, TILE:PAD] + pick_right(narrow[:, 0:WIDTH], plain_lanes[...])
     inner_xr = times(inner_rows[...], inner_forward, whole)
 
     def elastic(g, lam, mu, sy, sx, sr, jw):
@@ -443,7 +448,8 @@
     valid = (iota((5, PAD), 1) < NODES) & (iota((5, PAD), 0) < 5)
     for e in range(ne):
         def plain(f):
-            return copies[slot(f, e) : slot(f, e) + 5, :]
+            at = slice(slot(f, e), slot(f, e) + 5)
+            return jnp.concatenate([narrow[at, 0:TILE], copies[at, :]], axis=1)
 
         def x_of(f):
             return slopes_xr[slot(f, e) : slot(f, e) + 5, 0:PAD]
@@ -501,10 +507,11 @@
             inner_flux[at : at + 5, 2 * INNER_PAD : 2 * INNER_PAD + INNER_WIDTH] = along(slope_back, q[f][0])
 
     back = times(flux[:, 0 : 2 * PAD], forward, whole, back=True)
-    own_y = flux[:, 2 * PAD : 3 * PAD]
-    count = own_y.shape[0]
-    out = product(jnp.concatenate(parts_of(own_y), axis=0), plain_lanes[...], back=True)
-    back = back + (out[0:count] + out[count : 2 * count] + out[2 * count : 3 * count])
+    count = flux.shape[0]
+    out = product(
+        jnp.concatenate(parts_of(flux[:, 2 * PAD + TILE : 3 * PAD]), axis=0), plain_lanes[...], back=True
+    )
+    back = back + flux[:, 2 * PAD : 2 * PAD + WIDTH] + (out[0:count] + out[count : 2 * count] + out[2 * count : 3 * count])
     count = 3 * ne * 8
     stack[0:count, :] = (
         times(inner_flux[:, 0 : 2 * INNER_PAD], inner_forward, whole, back=True)
@@ -557,7 +564,8 @@
         last = edges[ypad : ypad + rows, p * 128 : p * 128 + 128]
         send_xa[p * rows : (p + 1) * rows, :] = jnp.where(even_x, last, first)
         send_xb[p * rows : (p + 1) * rows, :] = jnp.where(even_x, first, last)
-    rows_t[...] = jnp.zeros(rows_t.shape, jnp.float32)
+    rows_t[0:16, :] = jnp.zeros((16, PAD), jnp.float32)
+    rows_t[64:80, :] = jnp.zeros((16, PAD), jnp.float32)
     for f in range(FIELDS):
         rows_t[f : f + 1, :] = fields[f, rows - 1 : rows, :]
         rows_t[64 + f : 65 + f, :] = fields[f, 0:1, :]
@@ -613,6 +621,36 @@
         send_all[pl.ds(row, peers, stride=BLOCK), :] = block
 
 
+def window_kernel(
+    disp,
+    vel,
+    acc,
+    pot,
+    rate,
+    accel,
+    inner_disp,
+    inner_vel,
+    inner_acc,
+    fields,
+    disp_next,
+    pot_next,
+    inner_next,
+    vel_half,
+    rate_half,
+    inner_half,
+    fields_out,
+):
+    half = 0.5 * time_step
+    for new, between, place, speed, change in (
+        (disp_next, vel_half, disp, vel, acc),
+        (pot_next, rate_half, pot, rate, accel),
+        (inner_next, inner_half, inner_disp, inner_vel, inner_acc),
+    ):
+        new[...] = place[...] + time_step * speed[...] + half * time_step * change[...]
+        between[...] = speed[...] + half * change[...]
+    fields_out[...] = fields[...]
+
+
 def close_kernel(
     rows,
     count_x,
@@ -623,12 +661,9 @@
     got_yb,
     got_all,
     fields,
-    vel,
-    acc,
-    rate,
-    accel,
-    inner_vel,
-    inner_acc,
+    vel_half,
+    rate_half,
+    inner_half,
     table_ref,
     pick,
     polar_back,
@@ -770,7 +805,7 @@
     inside = (lane < WIDTH) & (iota((ypad, PAD), 0) < rows)
     core = total[CF] / jnp.where(inside, total[CM], 1.0)
     accel_next[...] = core[0:rows, 0:WIDTH]
-    rate_next[...] = rate[...] + half * (accel[...] + core[0:rows, 0:WIDTH])
+    rate_next[...] = rate_half[...] + half * core[0:rows, 0:WIDTH]
     push = total[CW] * core
     top = jnp.where(radial == 0, pltpu.roll(push, PAD - (RADIAL - 1), axis=1), 0.0)
     bottom = jnp.where(radial == INNER_RADIAL - 1, pltpu.roll(push, INNER_RADIAL - 1, axis=1), 0.0)
@@ -786,10 +821,10 @@
     for y in range(rows):
         result = jnp.concatenate([wide[t, 4 * y : 4 * y + 3, :] for t in range(PAD // 128)], axis=1)[:, 0:WIDTH]
         acc_next[y] = result
-        vel_next[y] = vel[y] + half * (acc[y] + result)
+        vel_next[y] = vel_half[y] + half * result
         result = squeezed[4 * y : 4 * y + 3, :]
         inner_acc_next[y] = result
-        inner_vel_next[y] = inner_vel[y] + half * (inner_acc[y] + result)
+        inner_vel_next[y] = inner_half[y] + half * result
 
 
 def shards(
@@ -829,12 +864,9 @@
     shape = lambda *s: jax.ShapeDtypeStruct(s, f32)
     devices = count_x * count_y
     edge = -(-PAIRS * rows // 8) * 8
-    (mantle_next, core_next, inner_next, fields, xa, xb, ya, yb, everyone) = pl.pallas_call(
+    (fields, xa, xb, ya, yb, everyone) = pl.pallas_call(
         functools.partial(force_kernel, rows, count_x, count_y),
         out_shape=[
-            like(mantle_disp),
-            like(core_pot),
-            like(inner_disp),
             shape(FIELDS, ypad, PAD),
             shape(edge, 128),
             shape(edge, 128),
@@ -844,7 +876,7 @@
         ],
         scratch_shapes=[
             pltpu.VMEM((4 * ne * 8, WIDTH), f32),
-            pltpu.VMEM((13 * ne * 8, WIDTH), f32),
+            pltpu.VMEM((13 * ne * 8, PAD), f32),
             pltpu.VMEM((3 * ne * 8, INNER_WIDTH), f32),
             pltpu.VMEM((4 * ne * 8, 3 * PAD), f32),
             pltpu.VMEM((3 * ne * 8, 3 * INNER_PAD), f32),
@@ -856,7 +888,9 @@
         + [pltpu.VMEM((PAD // 128, 4 * rows, 128), f32)] * 4
         + [pltpu.VMEM((INNER_PAD // 128, 4 * rows, 128), f32)] * 3
         + [pltpu.VMEM((3 * ne * 8 + 2 * ypad, INNER_WIDTH), f32)]
-        + [pltpu.VMEM((ENTRIES, RUN_ROWS * 128), f32)],
+        + [pltpu.VMEM((ENTRIES, RUN_ROWS * 128), f32)]
+        + [pltpu.VMEM((13 * ne * 8, PAD - TILE), f32)]
+        + [pltpu.VMEM((rows, WIDTH), f32)],
         name="forces",
     )(
         mantle_disp,
@@ -897,6 +931,12 @@
     far = [(j, (j - 1 if j % 2 == 0 else j + 1) % count_y) for j in range(count_y)]
     ya = lax.ppermute(ya, "eta", near)
     yb = lax.ppermute(yb, "eta", far)
+    (mantle_next, core_next, inner_next, vel_half, rate_half, inner_half, fields) = pl.pallas_call(
+        window_kernel,
+        out_shape=[like(a) for a in (mantle_disp, core_pot, inner_disp) * 2] + [like(fields)],
+        compiler_params=pltpu.CompilerParams(vmem_limit_bytes=WINDOW_GRANT),
+        name="window",
+    )(mantle_disp, mantle_vel, mantle_acc, core_pot, core_rate, core_accel, inner_disp, inner_vel, inner_acc, fields)
     (mantle_vel_next, mantle_acc_next, core_rate_next, core_acc_next, inner_vel_next, inner_acc_next) = pl.pallas_call(
         functools.partial(close_kernel, rows, count_x, count_y),
         out_shape=[
@@ -925,12 +965,9 @@
         yb,
         everyone,
         fields,
-        mantle_vel,
-        mantle_acc,
-        core_rate,
-        core_accel,
-        inner_vel,
-        inner_acc,
+        vel_half,
+        rate_half,
+        inner_half,
         table,
         tables["pick"],
         tables["polar_back"],

time: 27.6 us -> 26.3 us (0.953)
  waiting for transfers between devices: 3.46 us -> 1.74 us
  Pallas kernels: 7.98 us -> 8.39 us
    ppermute x1, waiting for transfers between devices: 1.09 us -> 0.01 us  [shards(): ya = lax.ppermute(ya, 'eta', near)]
    pallas_call x0 -> x1, Pallas kernels: none -> 0.71 us  [shards(): pl.pallas_call(window_kernel, out_shape=[like(a) for a in (mantle_disp, c...]
    ppermute x1, waiting for transfers between devices: 2.37 us -> 1.73 us  [shards(): yb = lax.ppermute(yb, 'eta', far)]
    pallas_call x1, Pallas kernels: 5.85 us -> 5.52 us  [shards(): pl.pallas_call(functools.partial(force_kernel, rows, count_x, count_y), o...]
    unnamed x22 -> x28, local copies, waits for them, and re-layouts: 1 us -> 1.01 us
  transfers between devices with their start and end apart: 5 -> 5, of which waited for: 2 -> 1; matrix products, arithmetic and copies ran while one was open for 0% -> 0% of each run, Pallas kernels for 0% -> 3%
where the time goes in v1:
time: 26.3 us; the launch traced here: 26.1 us
  starting transfers between devices  14.1 us (54%)
  Pallas kernels  8.39 us (32%)
  waiting for transfers between devices  1.74 us (7%)
  local copies, waits for them, and re-layouts  1.01 us (4%)
  between operations  0.86 us (3%)
    all_to_all x1, starting transfers between devices, shards(): everyone = lax.all_to_all(everyone, ('xi', 'eta'), 0, 0, tiled=True)  7.33 us
    pallas_call x1, Pallas kernels, shards(): pl.pallas_call(functools.partial(force_kernel, rows, count_x, count_y), o...  5.52 us
    ppermute x1, starting transfers between devices, shards(): xb = lax.ppermute(xb, 'xi', far)  3.48 us
    pallas_call x1, Pallas kernels, shards(): pl.pallas_call(functools.partial(close_kernel, rows, count_x, count_y), o...  2.15 us
    ppermute x1, waiting for transfers between devices, shards(): yb = lax.ppermute(yb, 'eta', far)  1.73 us
    ppermute x1, starting transfers between devices, shards(): ya = lax.ppermute(ya, 'eta', near)  1.48 us
    ppermute x1, starting transfers between devices, shards(): yb = lax.ppermute(yb, 'eta', far)  1.48 us
    unnamed x28, local copies, waits for them, and re-layouts  1.01 us
  transfers between devices with their start and end apart: 5, of which 1 were waited for; matrix products, arithmetic and copies ran while one was open for 0% of the time, Pallas kernels for 3%

profile of v1, /device:TPU:0, one launch (start us, length us, event | category | flops | bytes accessed | tf_op | source)
XLA Modules:
  0.0 26.1 jit_solution(4401014637909332752)
XLA Ops:
  0.7 0.0 copy-start
  0.8 0.0 copy-start.1
  0.8 0.0 copy-start.2
  0.8 0.0 copy-start.7
  0.8 5.5 %forces.1 = (f32[11,16,384]{2,1,0:T(8,128)}, f32[56,128]{1,0:T(8,128)}, f32[56,128]{1,0:T(8,128)}, f32[16,384]{1,0:T(8,128)}, f32[16,384]{1,0:T(8,128)}, /*index=5*/f32[256,128]{1,0:T(8,128)}) custom-call(f32[9,3,270]{2,1,0:T(4,128)} %bitcast.20, f32[9,3,270]{2,1,0:T(4,128)} %bitcast.22, f32[9,3,270]{2,1,0:T(4,128)} %bitcast.24, f32[9,3,270]{2,1,0:T(4,128)} %bitcast.33, ...), custom_call_target="tpu_custom_call" | custom-call | tf_op jit(solution)/shard_map/forces/pallas_call | solution.py:867
  6.3 7.3 %all-to-all-start = ((f32[32,8,128]{2,1,0:T(8,128)}), f32[32,8,128]{2,1,0:T(8,128)S(1)}, u32[]{:S(2)}, u32[]{:S(2)}) async-start(f32[32,8,128]{2,1,0:T(8,128)} %bitcast.32), calls=%async_computation | async-start | bytes 262144 | tf_op jit(solution)/shard_map/all_to_all | solution.py:925
  13.7 0.3 %collective-permute-start = (f32[56,128]{1,0:T(8,128)}, f32[56,128]{1,0:T(8,128)S(1)}, u32[]{:S(2)}, u32[]{:S(2)}) collective-permute-start(f32[56,128]{1,0:T(8,128)} %get-tuple-element.30), channel_id=1, source_target_pairs={{0,4},{4,0},{8,12},{12,8},{16,20},{20,16},{24,28},{28,24},{1,5},{5... | collective-permute-start | bytes 86024 | tf_op jit(solution)/shard_map/ppermute | solution.py:928
  14.0 3.5 %collective-permute-start.1 = (f32[56,128]{1,0:T(8,128)}, f32[56,128]{1,0:T(8,128)S(1)}, u32[]{:S(2)}, u32[]{:S(2)}) collective-permute-start(f32[56,128]{1,0:T(8,128)} %get-tuple-element.31), channel_id=1, source_target_pairs={{0,28},{4,8},{8,4},{12,16},{16,12},{20,24},{24,20},{28,0},{1,29},{... | collective-permute-start | bytes 86024 | tf_op jit(solution)/shard_map/ppermute | solution.py:929
  17.5 1.5 %collective-permute-start.2 = (f32[16,384]{1,0:T(8,128)}, f32[16,384]{1,0:T(8,128)S(1)}, u32[]{:S(2)}, u32[]{:S(2)}) collective-permute-start(f32[16,384]{1,0:T(8,128)} %get-tuple-element.32), channel_id=1, source_target_pairs={{0,1},{1,0},{2,3},{3,2},{4,5},{5,4},{6,7},{7,6},{8,9},{9,8},{10,11... | collective-permute-start | bytes 73736 | tf_op jit(solution)/shard_map/ppermute | solution.py:932
  18.9 1.5 %collective-permute-start.3 = (f32[16,384]{1,0:T(8,128)}, f32[16,384]{1,0:T(8,128)S(1)}, u32[]{:S(2)}, u32[]{:S(2)}) collective-permute-start(f32[16,384]{1,0:T(8,128)} %get-tuple-element.33), channel_id=1, source_target_pairs={{0,3},{1,2},{2,1},{3,0},{4,7},{5,6},{6,5},{7,4},{8,11},{9,10},{10,... | collective-permute-start | bytes 73736 | tf_op jit(solution)/shard_map/ppermute | solution.py:933
  20.4 0.0 copy-done.4
  20.4 0.0 copy-done.9
  20.4 0.0 copy-done.10
  20.4 0.0 copy-done.11
  20.5 0.0 copy-done.12
  20.5 0.0 copy-done.13
  20.5 0.9 %copy-done.3 = f32[11,16,384]{2,1,0:T(8,128)S(1)} copy-done((f32[11,16,384]{2,1,0:T(8,128)S(1)}, f32[11,16,384]{2,1,0:T(8,128)}, u32[]{:S(2)}) %copy-start.3) | copy-done | bytes 270360
  21.4 0.7 %window.1 = (f32[9,3,270]{2,1,0:T(4,128)}, f32[9,270]{1,0:T(8,128)}, f32[9,3,150]{2,1,0:T(4,128)}, f32[9,3,270]{2,1,0:T(4,128)S(1)}, f32[9,270]{1,0:T(8,128)S(1)...) custom-call(f32[9,3,270]{2,1,0:T(4,128)S(1)} %bitcast.21, f32[9,3,270]{2,1,0:T(4,128)S(1)} %bitcast.23, ...), custom_call_target="tpu_custom_call" | custom-call | tf_op jit(solution)/shard_map/window/pallas_call | solution.py:934
  22.1 0.0 collective-permute-done.2.got_ya
  22.1 1.7 %collective-permute-done.3.got_yb = f32[16,384]{1,0:T(8,128)S(1)} collective-permute-done((f32[16,384]{1,0:T(8,128)}, f32[16,384]{1,0:T(8,128)S(1)}, u32[]{:S(2)}, u32[]{:S(2)}) %collective-permute-start.3) | collective-permute-done | bytes 24608 | tf_op jit(solution)/shard_map/ppermute | solution.py:933
  23.9 0.0 collective-permute-done.got_xa
  23.9 0.0 collective-permute-done.1.got_xb
  23.9 0.0 all-to-all-done
  23.9 2.2 %close.1 = (f32[9,3,270]{2,1,0:T(4,128)}, f32[9,3,270]{2,1,0:T(4,128)}, f32[9,270]{1,0:T(8,128)}, f32[9,270]{1,0:T(8,128)}, f32[9,3,150]{2,1,0:T(4,128)}, /*index=5*/f32[9,3,150]{2,1,0:T(4,128)}) custom-call(f32[56,128]{1,0:T(8,128)S(1)} %collective-permute-done.got_xa, f32[56,128]{1,0:T(8,128)S(1)} %collective-permute-done.1.got_xb, ...), custom_call_target="tpu_custom_call" | custom-call | tf_op jit(solution)/shard_map/close/pallas_call | solution.py:940
  (17 shorter events, 0.0 us)
Async XLA Ops:
  0.6 19.8 %copy-start.4 = (f32[3,9,270]{2,0,1:T(4,128)S(1)}, f32[3,9,270]{2,0,1:T(4,128)}, u32[]{:S(2)}) copy-start(f32[3,9,270]{2,0,1:T(4,128)} %param.30) | copy-start | bytes 87484
  0.7 19.8 %copy-start.5 = (f32[3,9,270]{2,0,1:T(4,128)S(1)}, f32[3,9,270]{2,0,1:T(4,128)}, u32[]{:S(2)}) copy-start(f32[3,9,270]{2,0,1:T(4,128)} %param.31) | copy-start | bytes 87484
  0.7 19.8 %copy-start.6 = (f32[3,9,270]{2,0,1:T(4,128)S(1)}, f32[3,9,270]{2,0,1:T(4,128)}, u32[]{:S(2)}) copy-start(f32[3,9,270]{2,0,1:T(4,128)} %param.32) | copy-start | bytes 87484
  0.7 19.7 %copy-start.8 = (f32[3,9,150]{2,0,1:T(4,128)S(1)}, f32[3,9,150]{2,0,1:T(4,128)}, u32[]{:S(2)}) copy-start(f32[3,9,150]{2,0,1:T(4,128)} %param.42) | copy-start | bytes 48604
  0.7 19.7 %copy-start.9 = (f32[3,9,150]{2,0,1:T(4,128)S(1)}, f32[3,9,150]{2,0,1:T(4,128)}, u32[]{:S(2)}) copy-start(f32[3,9,150]{2,0,1:T(4,128)} %param.43) | copy-start | bytes 48604
  0.7 19.7 %copy-start.10 = (f32[3,9,150]{2,0,1:T(4,128)S(1)}, f32[3,9,150]{2,0,1:T(4,128)}, u32[]{:S(2)}) copy-start(f32[3,9,150]{2,0,1:T(4,128)} %param.44) | copy-start | bytes 48604
  0.7 19.7 %copy-start.11 = (f32[9,270]{1,0:T(8,128)S(1)}, f32[9,270]{1,0:T(8,128)}, u32[]{:S(2)}) copy-start(f32[9,270]{1,0:T(8,128)} %pot.3) | copy-start | bytes 29164
  0.7 19.7 %copy-start.12 = (f32[9,270]{1,0:T(8,128)S(1)}, f32[9,270]{1,0:T(8,128)}, u32[]{:S(2)}) copy-start(f32[9,270]{1,0:T(8,128)} %rate.3) | copy-start | bytes 29164
  0.7 19.7 %copy-start.13 = (f32[9,270]{1,0:T(8,128)S(1)}, f32[9,270]{1,0:T(8,128)}, u32[]{:S(2)}) copy-start(f32[9,270]{1,0:T(8,128)} %accel.3) | copy-start | bytes 29164
  0.7 23.1 %copy-start = (bf16[288,384]{1,0:T(8,128)(2,1)S(1)}, bf16[288,384]{1,0:T(8,128)(2,1)}, u32[]{:S(2)}) copy-start(bf16[288,384]{1,0:T(8,128)(2,1)} %constant.32.clone.pick) | copy-start | bytes 663556
  0.8 23.1 %copy-start.1 = (f32[32,8,128]{2,1,0:T(8,128)S(1)}, f32[32,8,128]{2,1,0:T(8,128)}, u32[]{:S(2)}) copy-start(f32[32,8,128]{2,1,0:T(8,128)} %constant.35.clone.table_ref) | copy-start | bytes 393220
  0.8 23.1 %copy-start.2 = (bf16[256,768]{1,0:T(8,128)(2,1)S(1)}, bf16[256,768]{1,0:T(8,128)(2,1)}, u32[]{:S(2)}) copy-start(bf16[256,768]{1,0:T(8,128)(2,1)} %constant.34.clone.polar_back) | copy-start | bytes 1179652
  0.8 23.1 %copy-start.7 = (bf16[384,150]{1,0:T(8,128)(2,1)S(1)}, bf16[384,150]{1,0:T(8,128)(2,1)}, u32[]{:S(2)}) copy-start(bf16[384,150]{1,0:T(8,128)(2,1)} %constant.28.clone.squeeze) | copy-start | bytes 345604
  6.3 17.6 %all-to-all-start = ((f32[32,8,128]{2,1,0:T(8,128)}), f32[32,8,128]{2,1,0:T(8,128)S(1)}, u32[]{:S(2)}, u32[]{:S(2)}) async-start(f32[32,8,128]{2,1,0:T(8,128)} %bitcast.32), calls=%async_computation | async-start | bytes 262144 | tf_op jit(solution)/shard_map/all_to_all | solution.py:925
  13.7 10.2 %collective-permute-start = (f32[56,128]{1,0:T(8,128)}, f32[56,128]{1,0:T(8,128)S(1)}, u32[]{:S(2)}, u32[]{:S(2)}) collective-permute-start(f32[56,128]{1,0:T(8,128)} %get-tuple-element.30), channel_id=1, source_target_pairs={{0,4},{4,0},{8,12},{12,8},{16,20},{20,16},{24,28},{28,24},{1,5},{5... | collective-permute-start | bytes 86024 | tf_op jit(solution)/shard_map/ppermute | solution.py:928
  14.0 9.9 %collective-permute-start.1 = (f32[56,128]{1,0:T(8,128)}, f32[56,128]{1,0:T(8,128)S(1)}, u32[]{:S(2)}, u32[]{:S(2)}) collective-permute-start(f32[56,128]{1,0:T(8,128)} %get-tuple-element.31), channel_id=1, source_target_pairs={{0,28},{4,8},{8,4},{12,16},{16,12},{20,24},{24,20},{28,0},{1,29},{... | collective-permute-start | bytes 86024 | tf_op jit(solution)/shard_map/ppermute | solution.py:929
  17.5 4.7 %collective-permute-start.2 = (f32[16,384]{1,0:T(8,128)}, f32[16,384]{1,0:T(8,128)S(1)}, u32[]{:S(2)}, u32[]{:S(2)}) collective-permute-start(f32[16,384]{1,0:T(8,128)} %get-tuple-element.32), channel_id=1, source_target_pairs={{0,1},{1,0},{2,3},{3,2},{4,5},{5,4},{6,7},{7,6},{8,9},{9,8},{10,11... | collective-permute-start | bytes 73736 | tf_op jit(solution)/shard_map/ppermute | solution.py:932
  18.9 4.9 %collective-permute-start.3 = (f32[16,384]{1,0:T(8,128)}, f32[16,384]{1,0:T(8,128)S(1)}, u32[]{:S(2)}, u32[]{:S(2)}) collective-permute-start(f32[16,384]{1,0:T(8,128)} %get-tuple-element.33), channel_id=1, source_target_pairs={{0,3},{1,2},{2,1},{3,0},{4,7},{5,6},{6,5},{7,4},{8,11},{9,10},{10,... | collective-permute-start | bytes 73736 | tf_op jit(solution)/shard_map/ppermute | solution.py:933
  20.5 1.0 %copy-start.3 = (f32[11,16,384]{2,1,0:T(8,128)S(1)}, f32[11,16,384]{2,1,0:T(8,128)}, u32[]{:S(2)}) copy-start(f32[11,16,384]{2,1,0:T(8,128)} %get-tuple-element.28.fields) | copy-start | bytes 811012

commit v2 on v1

--- a/solution.py
+++ b/solution.py
@@ -72,6 +72,19 @@
     return weights, slopes
 
 
+def short_slopes():
+    slopes = gll_tables()[1]
+    round_bf16 = lambda v: float(np.float32(v).astype(jnp.bfloat16))
+    high = np.vectorize(round_bf16)(slopes)
+    low = np.vectorize(round_bf16)(slopes - high)
+    for a in range(5):
+        for _ in range(3):
+            for b in np.argsort(np.abs(low[a])):
+                excess = np.sum(high[a]) + np.sum(low[a])
+                low[a, b] = round_bf16(low[a, b] - excess)
+    return high + low
+
+
 def spread_table(count):
     spread = np.zeros((4 * count + 1, 5 * count))
     for element in range(count):
@@ -85,7 +98,7 @@
 
 
 def lane_tables(layers, width):
-    weights, slopes = gll_tables()
+    weights, slopes = gll_tables()[0], short_slopes()
     spread = spread_table(layers)
     derive = np.kron(np.eye(layers), slopes.T)
     eye_k = np.eye(GROUPS)
@@ -138,13 +151,20 @@
             for r in range(RADIAL):
                 if channel(r, f) is not None:
                     polar[(f // 2) * 128 + (f % 2) * 64 + k * RADIAL + r, (k - 4) * 128 + channel(r, f)] = 1.0
+    polar_short = np.zeros((2 * 128, 256))
+    for f in range(FIELDS):
+        for k in (4, 5):
+            for r in range(RADIAL):
+                if channel(r, f) is not None:
+                    row = (f // 6) * 128 + (f % 2) * 64 + (f // 2 % 3) * 2 * RADIAL + (k - 4) * RADIAL + r
+                    polar_short[row, (k - 4) * 128 + channel(r, f)] = 1.0
     as_f32 = lambda t: np.asarray(t, np.float32)
     as_bf16 = lambda t: np.asarray(t, np.float32).astype(bf16)
 
     def split(t):
         rest = as_f32(t)
         out = []
-        for _ in range(3):
+        for _ in range(2):
             out.append(rest.astype(bf16))
             rest = rest - out[-1].astype(np.float32)
         return np.stack(out)
@@ -159,7 +179,7 @@
         columns=as_f32(columns),
         along_y=as_f32(along_y),
         pick=as_bf16(pick),
-        polar=as_bf16(polar),
+        polar=as_bf16(polar_short),
         polar_back=as_bf16(polar.T),
     )
 
@@ -281,7 +301,7 @@
     total = out[0:count] + (out[count : 2 * count] + out[2 * count : 3 * count])
     out = product(jnp.concatenate([high, middle], axis=0), table[1, :, lanes], back)
     total = total + (out[0:count] + out[count : 2 * count])
-    return total + product(high, table[2, :, lanes], back)
+    return total
 
 
 def turn_lanes(x, shift):
@@ -591,7 +611,16 @@
             bottom_points = bottom_points + turn_lanes(lower, at - first - 64)
     points[0:32, :] = top_points
     points[32:64, :] = bottom_points
-    caps = pick_right(edges[...], polar[...])
+    third = lax.rem(iota((2 * ypad, 128), 1), 64)
+    tiles = []
+    for t in range(2):
+        tile = jnp.zeros((2 * ypad, 128), jnp.float32)
+        for j in range(3):
+            p = 3 * t + j
+            block = turn_lanes(edges[:, p * 128 : p * 128 + 128], 2 * RADIAL * j - 4 * RADIAL)
+            tile = jnp.where((third >= 2 * RADIAL * j) & (third < 2 * RADIAL * (j + 1)), block, tile)
+        tiles.append(tile)
+    caps = pick_right(jnp.concatenate(tiles, axis=1), polar[...])
     points[64 : 64 + 2 * ypad, :] = caps[:, 0:128]
     points[64 + 2 * ypad : 64 + 4 * ypad, :] = caps[:, 128:256]
 

time: 26.3 us -> 25.8 us (0.981)
  Pallas kernels: 8.39 us -> 7.87 us
    pallas_call x1, Pallas kernels: 5.52 us -> 5.01 us  [shards(): pl.pallas_call(functools.partial(force_kernel, rows, count_x, count_y), o...]
where the time goes in v2:
time: 25.8 us; the launch traced here: 25.5 us
  starting transfers between devices  14.1 us (55%)
  Pallas kernels  7.87 us (31%)
  waiting for transfers between devices  1.74 us (7%)
  local copies, waits for them, and re-layouts  1 us (4%)
  between operations  0.84 us (3%)
    all_to_all x1, starting transfers between devices, shards(): everyone = lax.all_to_all(everyone, ('xi', 'eta'), 0, 0, tiled=True)  7.33 us
    pallas_call x1, Pallas kernels, shards(): pl.pallas_call(functools.partial(force_kernel, rows, count_x, count_y), o...  5.01 us
    ppermute x1, starting transfers between devices, shards(): xb = lax.ppermute(xb, 'xi', far)  3.48 us
    pallas_call x1, Pallas kernels, shards(): pl.pallas_call(functools.partial(close_kernel, rows, count_x, count_y), o...  2.15 us
    ppermute x1, waiting for transfers between devices, shards(): yb = lax.ppermute(yb, 'eta', far)  1.73 us
    ppermute x1, starting transfers between devices, shards(): ya = lax.ppermute(ya, 'eta', near)  1.48 us
    ppermute x1, starting transfers between devices, shards(): yb = lax.ppermute(yb, 'eta', far)  1.48 us
    unnamed x28, local copies, waits for them, and re-layouts  1 us
  transfers between devices with their start and end apart: 5, of which 1 were waited for; matrix products, arithmetic and copies ran while one was open for 0% of the time, Pallas kernels for 3%

profile of v2, /device:TPU:0, one launch (start us, length us, event | category | flops | bytes accessed | tf_op | source)
XLA Modules:
  0.0 25.5 jit_solution(2737984676485127902)
XLA Ops:
  0.6 0.0 copy-start.4
  0.7 0.0 copy-start.7
  0.8 5.0 %forces.1 = (f32[11,16,384]{2,1,0:T(8,128)}, f32[56,128]{1,0:T(8,128)}, f32[56,128]{1,0:T(8,128)}, f32[16,384]{1,0:T(8,128)}, f32[16,384]{1,0:T(8,128)}, /*index=5*/f32[256,128]{1,0:T(8,128)}) custom-call(f32[9,3,270]{2,1,0:T(4,128)} %bitcast.20, f32[9,3,270]{2,1,0:T(4,128)} %bitcast.22, f32[9,3,270]{2,1,0:T(4,128)} %bitcast.24, f32[9,3,270]{2,1,0:T(4,128)} %bitcast.33, ...), custom_call_target="tpu_custom_call" | custom-call | tf_op jit(solution)/shard_map/forces/pallas_call | solution.py:896
  5.8 0.0 copy-start.2
  5.8 7.3 %all-to-all-start = ((f32[32,8,128]{2,1,0:T(8,128)}), f32[32,8,128]{2,1,0:T(8,128)S(1)}, u32[]{:S(2)}, u32[]{:S(2)}) async-start(f32[32,8,128]{2,1,0:T(8,128)} %bitcast.32), calls=%async_computation | async-start | bytes 262144 | tf_op jit(solution)/shard_map/all_to_all | solution.py:954
  13.1 0.3 %collective-permute-start = (f32[56,128]{1,0:T(8,128)}, f32[56,128]{1,0:T(8,128)S(1)}, u32[]{:S(2)}, u32[]{:S(2)}) collective-permute-start(f32[56,128]{1,0:T(8,128)} %get-tuple-element.30), channel_id=1, source_target_pairs={{0,4},{4,0},{8,12},{12,8},{16,20},{20,16},{24,28},{28,24},{1,5},{5... | collective-permute-start | bytes 86024 | tf_op jit(solution)/shard_map/ppermute | solution.py:957
  13.4 3.5 %collective-permute-start.1 = (f32[56,128]{1,0:T(8,128)}, f32[56,128]{1,0:T(8,128)S(1)}, u32[]{:S(2)}, u32[]{:S(2)}) collective-permute-start(f32[56,128]{1,0:T(8,128)} %get-tuple-element.31), channel_id=1, source_target_pairs={{0,28},{4,8},{8,4},{12,16},{16,12},{20,24},{24,20},{28,0},{1,29},{... | collective-permute-start | bytes 86024 | tf_op jit(solution)/shard_map/ppermute | solution.py:958
  16.9 1.5 %collective-permute-start.2 = (f32[16,384]{1,0:T(8,128)}, f32[16,384]{1,0:T(8,128)S(1)}, u32[]{:S(2)}, u32[]{:S(2)}) collective-permute-start(f32[16,384]{1,0:T(8,128)} %get-tuple-element.32), channel_id=1, source_target_pairs={{0,1},{1,0},{2,3},{3,2},{4,5},{5,4},{6,7},{7,6},{8,9},{9,8},{10,11... | collective-permute-start | bytes 73736 | tf_op jit(solution)/shard_map/ppermute | solution.py:961
  18.4 1.5 %collective-permute-start.3 = (f32[16,384]{1,0:T(8,128)}, f32[16,384]{1,0:T(8,128)S(1)}, u32[]{:S(2)}, u32[]{:S(2)}) collective-permute-start(f32[16,384]{1,0:T(8,128)} %get-tuple-element.33), channel_id=1, source_target_pairs={{0,3},{1,2},{2,1},{3,0},{4,7},{5,6},{6,5},{7,4},{8,11},{9,10},{10,... | collective-permute-start | bytes 73736 | tf_op jit(solution)/shard_map/ppermute | solution.py:962
  19.9 0.0 copy-done.8
  19.9 0.0 copy-done.9
  19.9 0.0 copy-done.10
  19.9 0.0 copy-done.11
  19.9 0.0 copy-done.12
  19.9 0.0 copy-done.13
  19.9 0.0 copy-start.3
  20.0 0.9 %copy-done.3 = f32[11,16,384]{2,1,0:T(8,128)S(1)} copy-done((f32[11,16,384]{2,1,0:T(8,128)S(1)}, f32[11,16,384]{2,1,0:T(8,128)}, u32[]{:S(2)}) %copy-start.3) | copy-done | bytes 270360
  20.9 0.7 %window.1 = (f32[9,3,270]{2,1,0:T(4,128)}, f32[9,270]{1,0:T(8,128)}, f32[9,3,150]{2,1,0:T(4,128)}, f32[9,3,270]{2,1,0:T(4,128)S(1)}, f32[9,270]{1,0:T(8,128)S(1)...) custom-call(f32[9,3,270]{2,1,0:T(4,128)S(1)} %bitcast.21, f32[9,3,270]{2,1,0:T(4,128)S(1)} %bitcast.23, ...), custom_call_target="tpu_custom_call" | custom-call | tf_op jit(solution)/shard_map/window/pallas_call | solution.py:963
  21.6 0.0 collective-permute-done.2.got_ya
  21.6 1.7 %collective-permute-done.3.got_yb = f32[16,384]{1,0:T(8,128)S(1)} collective-permute-done((f32[16,384]{1,0:T(8,128)}, f32[16,384]{1,0:T(8,128)S(1)}, u32[]{:S(2)}, u32[]{:S(2)}) %collective-permute-start.3) | collective-permute-done | bytes 24608 | tf_op jit(solution)/shard_map/ppermute | solution.py:962
  23.3 0.0 collective-permute-done.got_xa
  23.3 0.0 collective-permute-done.1.got_xb
  23.3 0.0 all-to-all-done
  23.4 2.2 %close.1 = (f32[9,3,270]{2,1,0:T(4,128)}, f32[9,3,270]{2,1,0:T(4,128)}, f32[9,270]{1,0:T(8,128)}, f32[9,270]{1,0:T(8,128)}, f32[9,3,150]{2,1,0:T(4,128)}, /*index=5*/f32[9,3,150]{2,1,0:T(4,128)}) custom-call(f32[56,128]{1,0:T(8,128)S(1)} %collective-permute-done.got_xa, f32[56,128]{1,0:T(8,128)S(1)} %collective-permute-done.1.got_xb, ...), custom_call_target="tpu_custom_call" | custom-call | tf_op jit(solution)/shard_map/close/pallas_call | solution.py:969
  (17 shorter events, 0.0 us)
Async XLA Ops:
  0.6 19.2 %copy-start.4 = (f32[3,9,270]{2,0,1:T(4,128)S(1)}, f32[3,9,270]{2,0,1:T(4,128)}, u32[]{:S(2)}) copy-start(f32[3,9,270]{2,0,1:T(4,128)} %param.30) | copy-start | bytes 87484
  0.7 19.2 %copy-start.5 = (f32[3,9,270]{2,0,1:T(4,128)S(1)}, f32[3,9,270]{2,0,1:T(4,128)}, u32[]{:S(2)}) copy-start(f32[3,9,270]{2,0,1:T(4,128)} %param.31) | copy-start | bytes 87484
  0.7 19.2 %copy-start.6 = (f32[3,9,270]{2,0,1:T(4,128)S(1)}, f32[3,9,270]{2,0,1:T(4,128)}, u32[]{:S(2)}) copy-start(f32[3,9,270]{2,0,1:T(4,128)} %param.32) | copy-start | bytes 87484
  0.7 19.2 %copy-start.8 = (f32[3,9,150]{2,0,1:T(4,128)S(1)}, f32[3,9,150]{2,0,1:T(4,128)}, u32[]{:S(2)}) copy-start(f32[3,9,150]{2,0,1:T(4,128)} %param.42) | copy-start | bytes 48604
  0.7 19.2 %copy-start.9 = (f32[3,9,150]{2,0,1:T(4,128)S(1)}, f32[3,9,150]{2,0,1:T(4,128)}, u32[]{:S(2)}) copy-start(f32[3,9,150]{2,0,1:T(4,128)} %param.43) | copy-start | bytes 48604
  0.7 19.2 %copy-start.10 = (f32[3,9,150]{2,0,1:T(4,128)S(1)}, f32[3,9,150]{2,0,1:T(4,128)}, u32[]{:S(2)}) copy-start(f32[3,9,150]{2,0,1:T(4,128)} %param.44) | copy-start | bytes 48604
  0.7 19.2 %copy-start.11 = (f32[9,270]{1,0:T(8,128)S(1)}, f32[9,270]{1,0:T(8,128)}, u32[]{:S(2)}) copy-start(f32[9,270]{1,0:T(8,128)} %pot.3) | copy-start | bytes 29164
  0.7 19.2 %copy-start.12 = (f32[9,270]{1,0:T(8,128)S(1)}, f32[9,270]{1,0:T(8,128)}, u32[]{:S(2)}) copy-start(f32[9,270]{1,0:T(8,128)} %rate.3) | copy-start | bytes 29164
  0.7 19.2 %copy-start.13 = (f32[9,270]{1,0:T(8,128)S(1)}, f32[9,270]{1,0:T(8,128)}, u32[]{:S(2)}) copy-start(f32[9,270]{1,0:T(8,128)} %accel.3) | copy-start | bytes 29164
  0.7 22.6 %copy-start.7 = (bf16[384,150]{1,0:T(8,128)(2,1)S(1)}, bf16[384,150]{1,0:T(8,128)(2,1)}, u32[]{:S(2)}) copy-start(bf16[384,150]{1,0:T(8,128)(2,1)} %constant.28.clone.squeeze) | copy-start | bytes 345604
  5.8 17.6 %copy-start.2 = (bf16[256,768]{1,0:T(8,128)(2,1)S(1)}, bf16[256,768]{1,0:T(8,128)(2,1)}, u32[]{:S(2)}) copy-start(bf16[256,768]{1,0:T(8,128)(2,1)} %constant.34.clone.polar_back) | copy-start | bytes 1179652
  5.8 17.6 %all-to-all-start = ((f32[32,8,128]{2,1,0:T(8,128)}), f32[32,8,128]{2,1,0:T(8,128)S(1)}, u32[]{:S(2)}, u32[]{:S(2)}) async-start(f32[32,8,128]{2,1,0:T(8,128)} %bitcast.32), calls=%async_computation | async-start | bytes 262144 | tf_op jit(solution)/shard_map/all_to_all | solution.py:954
  13.1 10.2 %collective-permute-start = (f32[56,128]{1,0:T(8,128)}, f32[56,128]{1,0:T(8,128)S(1)}, u32[]{:S(2)}, u32[]{:S(2)}) collective-permute-start(f32[56,128]{1,0:T(8,128)} %get-tuple-element.30), channel_id=1, source_target_pairs={{0,4},{4,0},{8,12},{12,8},{16,20},{20,16},{24,28},{28,24},{1,5},{5... | collective-permute-start | bytes 86024 | tf_op jit(solution)/shard_map/ppermute | solution.py:957
  13.4 9.9 %collective-permute-start.1 = (f32[56,128]{1,0:T(8,128)}, f32[56,128]{1,0:T(8,128)S(1)}, u32[]{:S(2)}, u32[]{:S(2)}) collective-permute-start(f32[56,128]{1,0:T(8,128)} %get-tuple-element.31), channel_id=1, source_target_pairs={{0,28},{4,8},{8,4},{12,16},{16,12},{20,24},{24,20},{28,0},{1,29},{... | collective-permute-start | bytes 86024 | tf_op jit(solution)/shard_map/ppermute | solution.py:958
  16.9 4.7 %collective-permute-start.2 = (f32[16,384]{1,0:T(8,128)}, f32[16,384]{1,0:T(8,128)S(1)}, u32[]{:S(2)}, u32[]{:S(2)}) collective-permute-start(f32[16,384]{1,0:T(8,128)} %get-tuple-element.32), channel_id=1, source_target_pairs={{0,1},{1,0},{2,3},{3,2},{4,5},{5,4},{6,7},{7,6},{8,9},{9,8},{10,11... | collective-permute-start | bytes 73736 | tf_op jit(solution)/shard_map/ppermute | solution.py:961
  18.4 4.9 %collective-permute-start.3 = (f32[16,384]{1,0:T(8,128)}, f32[16,384]{1,0:T(8,128)S(1)}, u32[]{:S(2)}, u32[]{:S(2)}) collective-permute-start(f32[16,384]{1,0:T(8,128)} %get-tuple-element.33), channel_id=1, source_target_pairs={{0,3},{1,2},{2,1},{3,0},{4,7},{5,6},{6,5},{7,4},{8,11},{9,10},{10,... | collective-permute-start | bytes 73736 | tf_op jit(solution)/shard_map/ppermute | solution.py:962
  19.9 1.0 %copy-start.3 = (f32[11,16,384]{2,1,0:T(8,128)S(1)}, f32[11,16,384]{2,1,0:T(8,128)}, u32[]{:S(2)}) copy-start(f32[11,16,384]{2,1,0:T(8,128)} %get-tuple-element.28.fields) | copy-start | bytes 811012
  20.9 2.5 %copy-start = (bf16[288,384]{1,0:T(8,128)(2,1)S(1)}, bf16[288,384]{1,0:T(8,128)(2,1)}, u32[]{:S(2)}) copy-start(bf16[288,384]{1,0:T(8,128)(2,1)} %constant.32.clone.pick) | copy-start | bytes 663556
  20.9 2.5 %copy-start.1 = (f32[32,8,128]{2,1,0:T(8,128)S(1)}, f32[32,8,128]{2,1,0:T(8,128)}, u32[]{:S(2)}) copy-start(f32[32,8,128]{2,1,0:T(8,128)} %constant.35.clone.table_ref) | copy-start | bytes 393220
